TPU v7x, 256 devices: a whole 4x4x8 slice. The times are simulated.
256 devices in a mesh: member: 16 (over z, y_lo), tile: 8 (over x, core), batch: 2 (over y_hi).
Axes of the slice: x: 4, y: 4 (y_hi: 2, y_lo: 2; y = y_hi * 2 + y_lo), z: 8, core: 2. Of those that a mesh axis runs over, the one named last changes fastest.
Arguments:
- latent: bfloat16 [16, 2, 8192, 1024], P('member', 'batch', 'tile'), may hold values from -6 to 6
- w_in: bfloat16 [1024, 1024], replicated, may hold values from -0.1875 to 0.1875
- w_out: bfloat16 [1024, 112], replicated, may hold values from -0.1875 to 0.1875
- observed: bfloat16 [2, 1024, 1792], P('batch', 'tile'), may hold values from -5 to 5
- patch_index: int32 [2, 512], P('batch', 'tile'), may hold values from 0 to 127
- counts: int32 [2, 512], P('batch', 'tile'), may hold values from 1 to 8
Outputs:
- grad_w1: float32 [1024, 1024], P(('member', 'tile', 'batch'))
- grad_w2: float32 [1024, 112], P(('member', 'tile', 'batch'))
Inputs may be any that keep to these rules, and one draw needn't show every extreme that they name: `patch_index`: a candidate of the same tile and lead time.
All inputs are finite; a program needn't handle non-finite values.
Results may differ from a plain program's by a relative error of at most 0.0017.
Values sent between devices are 32-bit elements; how exact they have to be, the bound alone decides.
A program may use at most 64 MiB of HBM per device.

v0:
```python
import jax
import jax.numpy as jnp
from jax import lax
from jax.sharding import Mesh
from jax.sharding import PartitionSpec as P

PATCH = 16
MEMBER = ("member_0", "member_1")
MEMBER_TILE_BATCH = ("member_0", "member_1", "tile", "batch")


def sum_by_axis(subtotal, axes):
    for axis in axes:
        subtotal = lax.psum_scatter(subtotal, axis, scatter_dimension=0, tiled=True)
    return subtotal


def in_blocks(shard, dim, count):
    shape = shard.shape
    parts = shard.reshape(*shape[:dim], count, shape[dim] // count, *shape[dim + 1 :])
    return jnp.moveaxis(parts, dim, 0)


def summed_on_arrival(shard, axis, dim):
    count = lax.axis_size(axis)
    parts = lax.all_to_all(in_blocks(shard, dim, count), axis, 0, 0, tiled=True)
    return jnp.sum(parts, axis=0)


def smooth_grad(deltas):
    return deltas / jnp.sqrt(jnp.sum(deltas * deltas, axis=-1, keepdims=True) + 1.0)


def shards(latent, w_in, w_out, observed, patch_index, counts):
    rows_in = latent[0, 0]
    nrows = rows_in.shape[0]
    channels = w_out.shape[1]
    width = w_in.shape[1]
    members = lax.axis_size(MEMBER)
    preact = jnp.dot(rows_in, w_in, preferred_element_type=jnp.float32)
    hidden = jax.nn.silu(preact).astype(jnp.bfloat16)
    decoded = jnp.dot(hidden, w_out, preferred_element_type=jnp.float32)
    npatch = nrows // PATCH
    patches = decoded.reshape(npatch, PATCH * channels)
    blocks = patches.reshape(members, 1, npatch // members, PATCH * channels)
    grouped = lax.all_to_all(blocks, MEMBER, split_axis=0, concat_axis=1, tiled=True)
    deltas = grouped[:, :, None] - grouped[:, None, :]
    summed = jnp.sum(smooth_grad(deltas), axis=2)
    returned = lax.all_to_all(summed, MEMBER, split_axis=1, concat_axis=0, tiled=True)
    pair = returned.reshape(npatch, PATCH * channels)
    pool = observed[0]
    picked = patch_index[0]
    choose = (picked[:, None] == jnp.arange(pool.shape[0], dtype=jnp.int32)[None, :]).astype(
        jnp.bfloat16
    )
    target = jnp.dot(choose, pool, preferred_element_type=jnp.float32)
    own = smooth_grad(patches - target)
    weight = counts[0].astype(jnp.float32)[:, None]
    grad_patch = weight * (own / members - pair / (members * members))
    grad_out = grad_patch.reshape(nrows, channels).astype(jnp.bfloat16)
    grad_hidden = lax.dot_general(
        grad_out, w_out, (((1,), (1,)), ((), ())), preferred_element_type=jnp.float32
    )
    sigma = jax.nn.sigmoid(preact)
    grad_preact = (grad_hidden * sigma * (1.0 + preact * (1.0 - sigma))).astype(jnp.bfloat16)
    first = lax.dot_general(
        rows_in, grad_preact, (((0,), (0,)), ((), ())), preferred_element_type=jnp.float32
    )
    second = lax.dot_general(
        hidden, grad_out, (((0,), (0,)), ((), ())), preferred_element_type=jnp.float32
    )
    partial_value = sum_by_axis(jnp.concatenate([first, second], axis=1), MEMBER)
    totals = summed_on_arrival(partial_value, ("tile", "batch"), 0)
    return (totals[:, :width], totals[:, width:])


def solution(mesh):
    split = Mesh(
        mesh.devices.reshape(8, 2, mesh.shape["tile"], mesh.shape["batch"]),
        ("member_0", "member_1", "tile", "batch"),
    )
    placed = (
        P(MEMBER, "batch", "tile", None),
        P(),
        P(),
        P("batch", "tile", None),
        P("batch", "tile"),
        P("batch", "tile"),
    )
    return jax.shard_map(
        shards,
        mesh=split,
        in_specs=placed,
        out_specs=(P(MEMBER_TILE_BATCH, None), P(MEMBER_TILE_BATCH, None)),
        check_vma=False,
    )
```

profile of v0, /device:TPU:1, one launch (start us, length us, event | category | flops | bytes accessed | tf_op | source)
XLA Modules:
  0.0 186.4 jit_solution(12944572019511777703)
XLA Ops:
  7.2 0.0 copy-start
  7.2 0.0 copy-start.2
  7.2 1.6 copy-done
  8.8 6.2 %multiply_convert_fusion.1 = (bf16[1024,1024]{1,0:T(8,128)(2,1)S(1)}, f32[1024,1024]{1,0:T(8,128)}) fusion(bf16[1024,1024]{1,0:T(8,128)(2,1)} %param.7, bf16[1,1,1024,1024]{3,2,1,0:T(8,128)(2,1)S(1)} %copy-done), kind=kOutput, calls=%fused_computation.6 | convolution fusion | flops 2152726528 | bytes 10485760 | tf_op jit(solution)/shard_map/dot_general | solution.py:40
  14.9 0.0 copy-start.1
  14.9 1.3 copy-done.1
  16.3 0.0 copy-done.2
  16.3 0.7 fusion.8
  17.0 0.0 copy-start.5
  17.0 0.0 copy-start.4
  17.0 0.5 reshape_reshape.3
  17.5 24.5 %all_to_all.23 = f32[16,1,4,1792]{3,2,1,0:T(4,128)S(1)} all-to-all(f32[16,1,4,1792]{3,2,1,0:T(4,128)S(1)} %bitcast.35), channel_id=1, replica_groups=mesh['member_0'=8,'member_1'=2,'tile'=8,'batch'=2] {'member_0','member_1'}, dimensions={0} | all-to-all | bytes 917504 | tf_op jit(solution)/shard_map/all_to_all | solution.py:46
  42.0 0.1 copy.18
  42.1 0.8 fusion.1
  42.9 2.9 %fusion = f32[16,4,1792]{2,1,0:T(4,128)} fusion(f32[16,16,4]{1,2,0:T(4,128)S(1)} %add_sqrt_fusion, f32[16,4,1792]{2,0,1:T(8,128)S(1)} %copy.18, f32[16,4,1792]{2,1,0:T(4,128)S(1)} %bitcast.34), kind=kLoop, calls=%fused_computation.2 | loop fusion | flops 5390336 | bytes 1380352 | tf_op jit(solution)/shard_map/reduce_sum | solution.py:48
  45.8 4.4 %all-to-all-start.1 = ((f32[1,16,4,1792]{3,2,0,1:T(4,128)}), f32[1,16,4,1792]{3,2,0,1:T(4,128)S(1)}, u32[]{:S(2)}, u32[]{:S(2)}) async-start(f32[1,16,4,1792]{3,2,0,1:T(4,128)} %bitcast.7), calls=%async_computation.1 | async-start | bytes 917504 | tf_op jit(solution)/shard_map/all_to_all | solution.py:49
  50.3 0.0 reduce-scatter.5.cloned.1.call-start
  50.3 0.2 reshape.68
  50.6 0.0 copy-done.5
  50.6 0.0 copy-done.4
  50.6 1.4 multiply_reduce_fusion
  52.0 12.8 %all-to-all-done.1 = f32[1,16,4,1792]{3,2,0,1:T(4,128)S(1)} async-done(((f32[1,16,4,1792]{3,2,0,1:T(4,128)}), f32[1,16,4,1792]{3,2,0,1:T(4,128)S(1)}, u32[]{:S(2)}, u32[]{:S(2)}) %all-to-all-start.1) | async-done | bytes 458784 | tf_op jit(solution)/shard_map/all_to_all | solution.py:49
  64.8 0.1 broadcast_multiply_fusion
  64.9 0.2 div.52
  65.0 0.0 copy-start.3
  65.0 0.1 multiply_convert_fusion.2
  65.2 0.4 convert_element_type.27
  65.6 2.1 %fusion.9 = f32[1024,112]{0,1:T(8,128)S(1)} fusion(bf16[1024,1024]{1,0:T(8,128)(2,1)} %copy-done.1, bf16[1024,112]{1,0:T(8,128)(2,1)S(1)} %convert_element_type.27), kind=kOutput, calls=%fused_computation.24 | convolution fusion | flops 234881024 | bytes 2785280 | tf_op jit(solution)/shard_map/dot_general | solution.py:69
  67.7 0.0 copy-done.3
  67.7 7.9 %convolution_bitcast_fusion = f32[1024,1024]{0,1:T(8,128)} fusion(bf16[1,1,1024,1024]{3,2,1,0:T(8,128)(2,1)S(1)} %copy-done, f32[1024,1024]{1,0:T(8,128)} %get-tuple-element.3, bf16[1024,112]{1,0:T(8,128)(2,1)S(1)} %convert_element_type.27, bf16[1024,112]{0,1:T(8,128)(2,1)S(1)} %copy-done.3), kind=kOutput, calls=%fused_computation.9 | convolution fusion | flops 2391801856 | bytes 10944512 | tf_op jit(solution)/shard_map/dot_general | solution.py:66
  75.5 5.0 %pad_maximum_fusion = f32[1024,1136]{0,1:T(8,128)} fusion(f32[1024,112]{0,1:T(8,128)S(1)} %fusion.9, f32[1024,1024]{0,1:T(8,128)} %convolution_bitcast_fusion), kind=kLoop, calls=%fused_computation.4 | loop fusion | flops 1163264 | bytes 9306112 | tf_op jit(solution)/shard_map/concatenate | solution.py:72
  80.5 0.0 reduce-scatter.5.cloned.1.call-update
  80.5 0.0 reduce-scatter.7.cloned.1.call-start
  80.6 58.4 %reduce-scatter.5.cloned.1.call-done = f32[128,1136]{0,1:T(8,128)} async-done(((f32[1024,1136]{0,1:T(8,128)}), f32[128,1136]{0,1:T(8,128)}) %reduce-scatter.5.cloned.1.call-update) | async-done | bytes 581648 | tf_op jit(solution)/shard_map/reduce_scatter | solution.py:14
  139.0 2.1 %copy.22 = f32[128,1136]{1,0:T(8,128)} copy(f32[128,1136]{0,1:T(8,128)} %reduce-scatter.5.cloned.1.call-done) | data formatting | bytes 1163264
  141.1 0.0 reduce-scatter.7.cloned.1.call-update
  141.1 19.4 %reduce-scatter.7.cloned.1.call-done = f32[64,1136]{1,0:T(8,128)} async-done(((f32[128,1136]{1,0:T(8,128)}), f32[64,1136]{1,0:T(8,128)}) %reduce-scatter.7.cloned.1.call-update) | async-done | bytes 290832 | tf_op jit(solution)/shard_map/reduce_scatter | solution.py:14
  160.5 1.0 reshape.69
  161.6 16.7 %all_to_all.24 = f32[16,4,1136]{2,1,0:T(4,128)S(1)} all-to-all(f32[16,4,1136]{2,1,0:T(4,128)S(1)} %reshape.69), channel_id=1, replica_groups=mesh['member_0'=8,'member_1'=2,'tile'=8,'batch'=2] {'tile','batch'}, dimensions={0} | all-to-all | bytes 581632 | tf_op jit(solution)/shard_map/all_to_all | solution.py:26
  178.3 0.1 reduce_sum.42
  178.4 0.6 slice.9
  178.9 0.6 slice.8
  (3 shorter events, 0.0 us)
Async XLA Ops:
  7.2 1.6 copy-start
  7.2 9.1 %copy-start.2 = (bf16[1024,112]{0,1:T(8,128)(2,1)S(1)}, bf16[1024,112]{0,1:T(8,128)(2,1)}, u32[]{:S(2)}) copy-start(bf16[1024,112]{0,1:T(8,128)(2,1)} %param.8) | copy-start | bytes 688132
  14.9 1.3 copy-start.1
  17.0 33.6 %copy-start.5 = (s32[1,64]{1,0:T(1,128)S(1)}, s32[1,64]{1,0:T(1,128)}, u32[]{:S(2)}) copy-start(s32[1,64]{1,0:T(1,128)} %param.11) | copy-start | bytes 772
  17.0 33.6 %copy-start.4 = (s32[1,64]{1,0:T(1,128)S(1)}, s32[1,64]{1,0:T(1,128)}, u32[]{:S(2)}) copy-start(s32[1,64]{1,0:T(1,128)} %param.10) | copy-start | bytes 772
  45.8 18.9 %all-to-all-start.1 = ((f32[1,16,4,1792]{3,2,0,1:T(4,128)}), f32[1,16,4,1792]{3,2,0,1:T(4,128)S(1)}, u32[]{:S(2)}, u32[]{:S(2)}) async-start(f32[1,16,4,1792]{3,2,0,1:T(4,128)} %bitcast.7), calls=%async_computation.1 | async-start | bytes 917504 | tf_op jit(solution)/shard_map/all_to_all | solution.py:49
  50.3 88.7 %reduce-scatter.5.cloned.1.call-start = ((), (), s32[]{:S(2)}) async-start(), calls=%async_computation.5 | async-start | bytes 5234688 | tf_op jit(solution)/shard_map/reduce_scatter | solution.py:14
  65.0 2.6 %copy-start.3 = (bf16[1024,112]{0,1:T(8,128)(2,1)S(1)}, bf16[1024,112]{0,1:T(8,128)(2,1)}, u32[]{:S(2)}) copy-start(bf16[1024,112]{0,1:T(8,128)(2,1)} %param.8) | copy-start | bytes 688132
  80.5 80.0 %reduce-scatter.7.cloned.1.call-start = ((), (), s32[]{:S(2)}) async-start(), calls=%async_computation.6 | async-start | bytes 884736 | tf_op jit(solution)/shard_map/reduce_scatter | solution.py:14
Sparse Core Ops, SparseCore 0:
  80.6 58.3 reduce-scatter.4
  141.5 18.9 reduce-scatter.6
where the time goes:
time: 187 us; the launch traced here: 186 us
  waiting for transfers between devices  90.6 us (48%)
  blocking collectives  41.2 us (22%)
  matrix products  18.2 us (10%)
  between operations  14.2 us (8%)
  other arithmetic  9.05 us (5%)
  local copies, waits for them, and re-layouts  8.6 us (5%)
  starting transfers between devices  4.52 us (2%)
    reduce_scatter x2, waiting for transfers between devices, sum_by_axis(): subtotal = lax.psum_scatter(subtotal, axis, scatter_dimension=0, tiled=True)  77.8 us
    all_to_all x1, blocking collectives, shards(): lax.all_to_all(blocks, MEMBER, split_axis=0, concat_axis=1, tiled=True)  24.5 us
    all_to_all x1, blocking collectives, summed_on_arrival(): parts = lax.all_to_all(in_blocks(shard, dim, count), axis, 0, 0, tiled=True)  16.7 us
    all_to_all x1, waiting for transfers between devices, shards(): lax.all_to_all(summed, MEMBER, split_axis=1, concat_axis=0, tiled=True)  12.8 us
    dot_general x1, matrix products, shards(): lax.dot_general(rows_in, grad_preact, (((0,), (0,)), ((), ())), preferred...  7.85 us
    dot_general x1, matrix products, shards(): preact = jnp.dot(rows_in, w_in, preferred_element_type=jnp.float32)  6.16 us
    unnamed x13, local copies, waits for them, and re-layouts  5.03 us
    concatenate x1, other arithmetic, shards(): jnp.concatenate([first, second], axis=1)  4.97 us
  transfers between devices with their start and end apart: 3, of which 3 were waited for; matrix products, arithmetic and copies ran while one was open for 1% of the time, Pallas kernels for 0%

commit v1 on v0

v1 whole, which is shorter than its diff:
```python
import jax
import jax.numpy as jnp
from jax import lax
from jax.experimental import pallas as pl
from jax.experimental.pallas import tpu as pltpu
from jax.sharding import PartitionSpec as P

MESH = pl.DeviceIdType.MESH
F32, BF16 = jnp.float32, jnp.bfloat16
ROWS, D, HID, CH, LANE = 1024, 1024, 1024, 112, 128
PATCH, NPATCH, MEMBERS, POOL, FEAT = 16, 64, 16, 128, 1792
NCHUNK, CROWS = 4, 256
ORDER = (1, 15, 2, 14, 3, 13, 4, 12, 5, 11, 6, 10, 7, 9, 8)
PAIRS = [(i, k) for i in range(MEMBERS) for k in range(i + 1, MEMBERS)]
PAIR_AT = {pair: at for at, pair in enumerate(PAIRS)}


def forward_chunk(c, lat, w_in, wo, pre, hid, dec):
    rows = pl.ds(pl.multiple_of(c * CROWS, CROWS), CROWS)
    for n in range(4):
        cols = slice(n * 256, n * 256 + 256)
        v = jnp.dot(lat[rows, :], w_in[:, cols], preferred_element_type=F32)
        pre[rows, cols] = v
        hid[rows, cols] = (v * (1.0 / (1.0 + jnp.exp(-v)))).astype(BF16)
    out = jnp.dot(hid[rows, :], wo[...], preferred_element_type=F32)
    dec[c] = out.reshape(MEMBERS, PATCH, LANE)


def slopes(pre):
    def step(i, carry):
        rows = pl.ds(pl.multiple_of(i * 64, 64), 64)
        v = pre[rows, :]
        sigma = 1.0 / (1.0 + jnp.exp(-v))
        pre[rows, :] = sigma * (1.0 + v * (1.0 - sigma))
        return carry

    lax.fori_loop(0, ROWS // 64, step, 0)


def transposed(src, dst):
    def step(i, carry):
        at = pl.ds(pl.multiple_of(i * 128, 128), 128)
        dst[at, :] = src[:, at].T
        return carry

    lax.fori_loop(0, 8, step, 0)


def own_term(obs, idx, cnt, dec, tgt, target, own, weight):
    pool_at = lax.broadcasted_iota(jnp.int32, (POOL, NPATCH), 0)
    choose = (pool_at == idx[...]).astype(F32).astype(BF16)
    picked = lax.dot_general(choose, obs[...], (((0,), (0,)), ((), ())), preferred_element_type=F32)
    tgt[...] = picked.astype(BF16)
    entry = lax.broadcasted_iota(jnp.int32, (256, LANE), 0)
    lane = lax.broadcasted_iota(jnp.int32, (256, LANE), 1)
    for i in range(PATCH):
        start = min(CH * i // 128 * 128, FEAT - 256)
        shift = ((entry == lane + (CH * i - start)) & (lane < CH)).astype(F32).astype(BF16)
        one = jnp.dot(tgt[:, start : start + 256], shift, preferred_element_type=F32)
        target[pl.ds(i, NPATCH, stride=PATCH), :] = one
    counts = cnt[...].astype(F32)

    def step(c, carry):
        rows = pl.ds(pl.multiple_of(c * CROWS, CROWS), CROWS)
        patch_of = (lax.broadcasted_iota(jnp.int32, (CROWS, NPATCH), 0) + c * CROWS) // PATCH
        at = lax.broadcasted_iota(jnp.int32, (CROWS, NPATCH), 1)
        count = jnp.sum(jnp.where(patch_of == at, counts, 0.0), axis=1, keepdims=True)
        delta = dec[c].reshape(CROWS, LANE) - target[rows, :]
        square = jnp.sum((delta * delta).reshape(MEMBERS, PATCH, LANE), axis=(1, 2), keepdims=True)
        scale = (1.0 / (MEMBERS * jnp.sqrt(square + 1.0))) * jnp.ones((MEMBERS, PATCH, LANE), F32)
        own[rows, :] = delta * scale.reshape(CROWS, LANE) * count
        weight[rows, :] = jnp.broadcast_to(count * (1.0 / (MEMBERS * MEMBERS)), (CROWS, LANE))
        return carry

    lax.fori_loop(0, NCHUNK, step, 0)


def pair_patch(c, x, part, inv, out):
    xs = [x[k, c] for k in range(MEMBERS)]
    for at, (i, k) in enumerate(PAIRS):
        d = xs[i] - xs[k]
        d = d * d
        part[at] = d[:8] + d[8:]
    total = jnp.sum(jnp.sum(part[...], axis=1), axis=1, keepdims=True)
    inv[...] = jnp.broadcast_to(1.0 / jnp.sqrt(total + 1.0), inv.shape)
    for i in range(MEMBERS):
        acc = None
        for k in range(MEMBERS):
            if k == i:
                continue
            at = PAIR_AT[(min(i, k), max(i, k))]
            term = (xs[i] - xs[k]) * inv[at : at + 1, :]
            acc = term if acc is None else acc + term
        out[c, i] = acc


def backward_chunk(c, back, own, weight, wo_t, slope, go, gp):
    rows = pl.ds(pl.multiple_of(c * CROWS, CROWS), CROWS)
    pair = back[c].reshape(CROWS, LANE)
    grad = (own[rows, :] - weight[rows, :] * pair).astype(BF16)
    go[rows, :] = grad
    for n in range(4):
        cols = slice(n * 256, n * 256 + 256)
        gh = jnp.dot(grad, wo_t[:, cols], preferred_element_type=F32)
        gp[rows, cols] = (gh * slope[rows, cols]).astype(BF16)


def halves(lo, hi):
    top = lax.broadcasted_iota(jnp.int32, lo.shape, lo.ndim - 2) < 4
    axis = lo.ndim - 2
    return jnp.where(top, lo, pltpu.roll(hi, 4, axis)), jnp.where(top, pltpu.roll(lo, 4, axis), hi)


def weight_grad(left, right, cols, half, put):
    def step(z, carry):
        at = pl.ds(pl.multiple_of(z * 128, 128), 128)
        g = jnp.dot(left[at, :], right[:, cols], preferred_element_type=F32)
        g = g.reshape(16, 8, g.shape[1])
        if half == 0:
            first, second = g, pltpu.roll(g, 4, 1)
        else:
            first, second = halves(g[:, :, :half], g[:, :, half:])
        for lo in range(2):
            for x in range(4):
                for core in range(2):
                    put(core, x, lo, z, first[(lo * 4 + x) * 2 + core])
                    put(core, x, 2 + lo, z, second[(lo * 4 + x) * 2 + core])
        return carry

    lax.fori_loop(0, 8, step, 0)


def kernel(
    lat_hbm, w_in_hbm, w_out_hbm, obs_hbm, idx_hbm, cnt_hbm, out1, out2,
    lat, w_in, w_raw, wo, wo_t, obs, idx, cnt, pre, hid, dec, x, tgt, target, own, weight, part, inv, ret, back,
    go, gp, lat_t, hid_t, qa, qb, qc, a0, b0, c0, a1, b1, c1, a2, b2, c2, a3, b3, c3,
    load_sem, there_send, there_recv, back_send, back_recv, rs_send, rs_recv,
):
    m, t, b = lax.axis_index("member"), lax.axis_index("tile"), lax.axis_index("batch")
    z, y_lo, xx, core = m // 2, m % 2, t // 2, t % 2
    y = b * 2 + y_lo

    def at_x(o):
        return {"tile": (xx + o) % 4 * 2 + core}

    def at_y(o):
        to = (y + o) % 4
        return {"member": z * 2 + to % 2, "batch": to // 2}

    def at_z(o):
        return {"member": (z + o) % 8 * 2 + y_lo}

    def at_member(o):
        return {"member": (m + o) % MEMBERS}

    def at_core():
        return {"tile": xx * 2 + (1 - core)}

    barrier = pltpu.get_barrier_semaphore()
    peers = [at_member(o) for o in range(1, 16)] + [at_core()] + [at_x(o) for o in range(1, 4)]
    for peer in peers:
        pl.semaphore_signal(barrier, inc=1, device_id=peer, device_id_type=MESH)
    for o in (1, 2, 3):
        pl.semaphore_signal(barrier, inc=1, device_id=at_y(o), device_id_type=MESH)

    loads = [pltpu.make_async_copy(w_in_hbm, w_in, load_sem.at[0])]
    for c in range(NCHUNK):
        rows = pl.ds(c * CROWS, CROWS)
        loads.append(pltpu.make_async_copy(lat_hbm.at[0, 0, rows, :], lat.at[rows, :], load_sem.at[1 + c]))
    loads.append(pltpu.make_async_copy(w_out_hbm, w_raw, load_sem.at[5]))
    loads.append(pltpu.make_async_copy(obs_hbm.at[0], obs, load_sem.at[6]))
    loads.append(pltpu.make_async_copy(idx_hbm, idx, load_sem.at[7]))
    loads.append(pltpu.make_async_copy(cnt_hbm, cnt, load_sem.at[8]))
    for load in loads:
        load.start()
    wo[...] = jnp.zeros(wo.shape, wo.dtype)
    loads[5].wait()
    wo[:, :CH] = w_raw[...]
    for load in loads[:5]:
        load.wait()
    pl.semaphore_wait(barrier, len(peers) + 3)

    def there(c, o):
        return pltpu.make_async_remote_copy(
            src_ref=dec.at[c, (m + o) % MEMBERS], dst_ref=x.at[m, c],
            send_sem=there_send.at[c, o], recv_sem=there_recv.at[c, o],
            device_id=at_member(o), device_id_type=MESH,
        )

    def returned(c, o):
        return pltpu.make_async_remote_copy(
            src_ref=ret.at[c, (m + o) % MEMBERS], dst_ref=back.at[c, m],
            send_sem=back_send.at[c, o], recv_sem=back_recv.at[c, o],
            device_id=at_member(o), device_id_type=MESH,
        )

    def forward(c, carry):
        forward_chunk(c, lat, w_in, wo, pre, hid, dec)
        x[m, c] = dec[c, m]
        for o in ORDER:
            there(c, o).start()
        return carry

    lax.fori_loop(0, NCHUNK, forward, 0)

    for load in loads[6:]:
        load.wait()
    wo_t[...] = wo[...].T
    own_term(obs, idx, cnt, dec, tgt, target, own, weight)
    slopes(pre)
    transposed(hid, hid_t)
    transposed(lat, lat_t)

    def arrived(make):
        def step(c, carry):
            for o in range(1, MEMBERS):
                make(c, o).wait_recv()
            return carry

        return step

    lax.fori_loop(0, NCHUNK, arrived(there), 0)

    def score(c, carry):
        pair_patch(c, x, part, inv, ret)
        back[c, m] = ret[c, m]
        for o in ORDER:
            returned(c, o).start()
        return carry

    lax.fori_loop(0, NCHUNK, score, 0)

    def backward(c, carry):
        arrived(returned)(c, 0)
        backward_chunk(c, back, own, weight, wo_t, pre, go, gp)
        return carry

    lax.fori_loop(0, NCHUNK, backward, 0)

    slots = iter(range(45))

    def send(src, dst, device):
        at = next(slots)
        copy = pltpu.make_async_remote_copy(
            src_ref=src, dst_ref=dst, send_sem=rs_send.at[at], recv_sem=rs_recv.at[at],
            device_id=device, device_id_type=MESH,
        )
        copy.start()
        sent.append(copy)
        return copy

    sent = []

    def added(own_ref, landed, copies):
        for copy in copies:
            copy.wait_recv()
        n = own_ref.shape[0]

        def step(i, carry):
            total = own_ref[i]
            for j in range(landed.shape[0]):
                total = total + landed[j, i]
            own_ref[i] = total
            return carry

        lax.fori_loop(0, n, step, 0)

    def put_a(k, x_, y_, z_, value):
        qa[k, x_, y_, z_] = value

    def put_b(k, x_, y_, z_, value):
        qb[k, y_, x_, z_] = value

    def put_c(k, x_, y_, z_, value):
        qc[k, z_, x_, y_] = value

    weight_grad(hid_t, go, slice(0, 128), 0, put_c)
    c_core = send(qc.at[1 - core], c0.at[0], at_core())
    weight_grad(lat_t, gp, slice(0, 512), 256, put_a)
    a_core = send(qa.at[1 - core], a0.at[0], at_core())
    added(qc.at[core], c0, [c_core])
    c_one = [send(qc.at[core, (z + o) % 8], c1.at[o - 1], at_z(o)) for o in (4, 3, 5, 2, 6, 1, 7)]
    weight_grad(lat_t, gp, slice(512, 1024), 256, put_b)
    b_core = send(qb.at[1 - core], b0.at[0], at_core())
    added(qa.at[core], a0, [a_core])
    a_one = [send(qa.at[core, (xx + o) % 4], a1.at[o - 1], at_x(o)) for o in (2, 1, 3)]
    added(qb.at[core], b0, [b_core])
    b_one = [send(qb.at[core, (y + o) % 4], b1.at[o - 1], at_y(o)) for o in (2, 1, 3)]
    added(qc.at[core, z], c1, c_one)
    c_two = [send(qc.at[core, z, (xx + o) % 4], c2.at[o - 1], at_x(o)) for o in (2, 1, 3)]
    added(qa.at[core, xx], a1, a_one)
    a_two = [send(qa.at[core, xx, (y + o) % 4], a2.at[o - 1], at_y(o)) for o in (2, 1, 3)]
    added(qb.at[core, y], b1, b_one)
    b_two = [send(qb.at[core, y, (xx + o) % 4], b2.at[o - 1], at_x(o)) for o in (2, 1, 3)]
    added(qc.at[core, z, xx], c2, c_two)
    c_three = [send(qc.at[core, z, xx, (y + o) % 4], c3.at[o - 1], at_y(o)) for o in (2, 1, 3)]
    added(qa.at[core, xx, y], a2, a_two)
    a_three = [send(qa.at[core, xx, y, (z + o) % 8], a3.at[o - 1], at_z(o)) for o in (4, 3, 5, 2, 6, 1, 7)]
    added(qb.at[core, y, xx], b2, b_two)
    b_three = [send(qb.at[core, y, xx, (z + o) % 8], b3.at[o - 1], at_z(o)) for o in (4, 3, 5, 2, 6, 1, 7)]

    def last(value, landed, copies):
        for copy in copies:
            copy.wait_recv()
        for j in range(landed.shape[0]):
            value = value + landed[j]
        return value

    total = last(qc[core, z, xx, y], c3, c_three)
    out2[...] = total[:4, :CH]
    total = last(qa[core, xx, y, z], a3, a_three)
    out1[:, 0:256] = total[:4]
    out1[:, 256:512] = pltpu.roll(total, 4, 0)[:4]
    total = last(qb[core, y, xx, z], b3, b_three)
    out1[:, 512:768] = total[:4]
    out1[:, 768:1024] = pltpu.roll(total, 4, 0)[:4]

    for copy in sent:
        copy.wait_send()

    def drained(c, carry):
        for o in range(1, MEMBERS):
            there(c, o).wait_send()
            returned(c, o).wait_send()
        return carry

    lax.fori_loop(0, NCHUNK, drained, 0)


def scratch():
    v = pltpu.VMEM
    return [
        v((ROWS, D), BF16), v((D, HID), BF16), v((HID, CH), BF16), v((HID, LANE), BF16), v((LANE, HID), BF16),
        v((POOL, FEAT), BF16), v((1, NPATCH), jnp.int32), v((1, NPATCH), jnp.int32),
        v((ROWS, HID), F32), v((ROWS, HID), BF16), v((NCHUNK, MEMBERS, PATCH, LANE), F32),
        v((MEMBERS, NCHUNK, PATCH, LANE), F32), v((NPATCH, FEAT), BF16), v((ROWS, LANE), F32),
        v((ROWS, LANE), F32), v((ROWS, LANE), F32), v((len(PAIRS), 8, LANE), F32), v((len(PAIRS), LANE), F32),
        v((NCHUNK, MEMBERS, PATCH, LANE), F32), v((NCHUNK, MEMBERS, PATCH, LANE), F32),
        v((ROWS, LANE), BF16), v((ROWS, HID), BF16), v((D, ROWS), BF16), v((HID, ROWS), BF16),
        v((2, 4, 4, 8, 8, 256), F32), v((2, 4, 4, 8, 8, 256), F32), v((2, 8, 4, 4, 8, 128), F32),
        v((1, 4, 4, 8, 8, 256), F32), v((1, 4, 4, 8, 8, 256), F32), v((1, 8, 4, 4, 8, 128), F32),
        v((3, 4, 8, 8, 256), F32), v((3, 4, 8, 8, 256), F32), v((7, 4, 4, 8, 128), F32),
        v((3, 8, 8, 256), F32), v((3, 8, 8, 256), F32), v((3, 4, 8, 128), F32),
        v((7, 8, 256), F32), v((7, 8, 256), F32), v((3, 8, 128), F32),
        pltpu.SemaphoreType.DMA((9,)),
        pltpu.SemaphoreType.DMA((NCHUNK, MEMBERS)), pltpu.SemaphoreType.DMA((NCHUNK, MEMBERS)),
        pltpu.SemaphoreType.DMA((NCHUNK, MEMBERS)), pltpu.SemaphoreType.DMA((NCHUNK, MEMBERS)),
        pltpu.SemaphoreType.DMA((45,)), pltpu.SemaphoreType.DMA((45,)),
    ]


def shards(latent, w_in, w_out, observed, patch_index, counts):
    return pl.pallas_call(
        kernel,
        out_shape=(jax.ShapeDtypeStruct((4, HID), F32), jax.ShapeDtypeStruct((4, CH), F32)),
        in_specs=[pl.BlockSpec(memory_space=pl.ANY)] * 6,
        out_specs=(pl.BlockSpec(memory_space=pltpu.VMEM), pl.BlockSpec(memory_space=pltpu.VMEM)),
        scratch_shapes=scratch(),
        compiler_params=pltpu.CompilerParams(
            collective_id=0, has_side_effects=True, vmem_limit_bytes=60 * 1024 * 1024
        ),
    )(latent, w_in, w_out, observed, patch_index, counts)


def solution(mesh):
    placed = (
        P("member", "batch", "tile", None),
        P(),
        P(),
        P("batch", "tile", None),
        P("batch", "tile"),
        P("batch", "tile"),
    )
    rows = P(("member", "tile", "batch"), None)
    return jax.shard_map(
        shards, mesh=mesh, in_specs=placed, out_specs=(rows, rows), check_vma=False
    )
```

time: 187 us -> 81.7 us (0.44)
  waiting for transfers between devices: 90.6 us -> 0 us
  Pallas kernels: 0 us -> 76.5 us
  blocking collectives: 41.2 us -> 0 us
  matrix products: 18.2 us -> 0 us
  between operations: 14.2 us -> 0.64 us
  other arithmetic: 9.05 us -> 0 us
  starting transfers between devices: 4.52 us -> 0 us
  local copies, waits for them, and re-layouts: 8.6 us -> 4.35 us
    reduce_scatter x2 -> x0, waiting for transfers between devices: 77.8 us -> none  [sum_by_axis(): subtotal = lax.psum_scatter(subtotal, axis, scatter_dimension=0, tiled=True)]
    pallas_call x0 -> x1, Pallas kernels: none -> 76.5 us  [shards(): pl.pallas_call(kernel, out_shape=(jax.ShapeDtypeStruct((4, HID), F32), ja...]
    all_to_all x2 -> x0, blocking collectives: 41.2 us -> none  [the longest x1 24.5 us: shards(): lax.all_to_all(blocks, MEMBER, split_axis=0, concat_axis=1, tiled=True)]
    dot_general x5 -> x0, matrix products: 18.2 us -> none  [the longest x1 7.85 us: shards(): lax.dot_general(rows_in, grad_preact, (((0,), (0,)), ((), ())), preferred...]
    all_to_all x1 -> x0, waiting for transfers between devices: 12.8 us -> none  [shards(): lax.all_to_all(summed, MEMBER, split_axis=1, concat_axis=0, tiled=True)]
    concatenate x1 -> x0, other arithmetic: 4.97 us -> none  [shards(): jnp.concatenate([first, second], axis=1)]
    all_to_all x1 -> x0, starting transfers between devices: 4.44 us -> none  [shards(): lax.all_to_all(summed, MEMBER, split_axis=1, concat_axis=0, tiled=True)]
    reduce_sum x3 -> x0, other arithmetic: 3.8 us -> none  [the longest x1 2.9 us: shards(): summed = jnp.sum(smooth_grad(deltas), axis=2)]
  transfers between devices with their start and end apart: 3 -> 0, of which waited for: 3 -> 0; matrix products, arithmetic and copies ran while one was open for 1% -> 0% of each run, Pallas kernels for 0% -> 0%
where the time goes in v1:
time: 81.7 us; the launch traced here: 81.5 us
  Pallas kernels  76.5 us (94%)
  local copies, waits for them, and re-layouts  4.35 us (5%)
    pallas_call x1, Pallas kernels, shards(): pl.pallas_call(kernel, out_shape=(jax.ShapeDtypeStruct((4, HID), F32), ja...  76.5 us
    unnamed x3, local copies, waits for them, and re-layouts  4.35 us

profile of v1, /device:TPU:1, one launch (start us, length us, event | category | flops | bytes accessed | tf_op | source)
XLA Modules:
  0.0 81.5 jit_solution(13486749766152309667)
XLA Ops:
  0.6 1.8 %copy.8.w_out_hbm = bf16[1024,112]{1,0:T(8,128)(2,1)} copy(bf16[1024,112]{0,1:T(8,128)(2,1)} %param.8) | data formatting | bytes 458752 | tf_op args[2]
  2.4 76.5 %shard_map.77 = (f32[4,1024]{1,0:T(4,128)}, f32[4,112]{1,0:T(4,128)}) custom-call(bf16[1,1,1024,1024]{3,2,1,0:T(8,128)(2,1)} %lat_hbm.1, bf16[1024,1024]{1,0:T(8,128)(2,1)} %w_in_hbm.1, bf16[1024,112]{1,0:T(8,128)(2,1)} %copy.8.w_out_hbm, bf16[1,128,1792]{2,1,0:T(8,128)(2,1)} %obs_hbm.1, s32[1,64]{1,0:T(1,128)} %idx_hbm.1, s32[1,64]{1,0:T(1,128)} %cnt_hbm.1), custom_call_target="tpu_custom_call" | custom-call | tf_op jit(solution)/shard_map/pallas_call | solution.py:353
  78.9 1.3 %copy.11 = f32[4,1024]{1,0:T(4,128)} copy(f32[4,1024]{1,0:T(4,128)} %get-tuple-element.4) | data formatting | bytes 32768
  80.3 1.3 %copy.12 = f32[4,112]{1,0:T(4,128)} copy(f32[4,112]{1,0:T(4,128)} %get-tuple-element.5) | data formatting | bytes 3584

commit v2 on v1

--- a/solution.py
+++ b/solution.py
@@ -17,11 +17,9 @@
 
 def forward_chunk(c, lat, w_in, wo, pre, hid, dec):
     rows = pl.ds(pl.multiple_of(c * CROWS, CROWS), CROWS)
-    for n in range(4):
-        cols = slice(n * 256, n * 256 + 256)
-        v = jnp.dot(lat[rows, :], w_in[:, cols], preferred_element_type=F32)
-        pre[rows, cols] = v
-        hid[rows, cols] = (v * (1.0 / (1.0 + jnp.exp(-v)))).astype(BF16)
+    v = jnp.dot(lat[rows, :], w_in[...], preferred_element_type=F32)
+    pre[rows, :] = v
+    hid[rows, :] = (v * (1.0 / (1.0 + jnp.exp(-v)))).astype(BF16)
     out = jnp.dot(hid[rows, :], wo[...], preferred_element_type=F32)
     dec[c] = out.reshape(MEMBERS, PATCH, LANE)
 
@@ -99,10 +97,19 @@
     pair = back[c].reshape(CROWS, LANE)
     grad = (own[rows, :] - weight[rows, :] * pair).astype(BF16)
     go[rows, :] = grad
-    for n in range(4):
-        cols = slice(n * 256, n * 256 + 256)
-        gh = jnp.dot(grad, wo_t[:, cols], preferred_element_type=F32)
-        gp[rows, cols] = (gh * slope[rows, cols]).astype(BF16)
+    gh = jnp.dot(grad, wo_t[...], preferred_element_type=F32)
+    gp[rows, :] = (gh * slope[rows, :]).astype(BF16)
+
+
+def accumulate(c, left, right, total):
+    rows = pl.ds(pl.multiple_of(c * CROWS, CROWS), CROWS)
+
+    def step(i, carry):
+        at = pl.ds(pl.multiple_of(i * 256, 256), 256)
+        total[at, :] += jnp.dot(left[at, rows], right[rows, :], preferred_element_type=F32)
+        return carry
+
+    lax.fori_loop(0, 4, step, 0)
 
 
 def halves(lo, hi):
@@ -111,29 +118,24 @@
     return jnp.where(top, lo, pltpu.roll(hi, 4, axis)), jnp.where(top, pltpu.roll(lo, 4, axis), hi)
 
 
-def weight_grad(left, right, cols, half, put):
-    def step(z, carry):
-        at = pl.ds(pl.multiple_of(z * 128, 128), 128)
-        g = jnp.dot(left[at, :], right[:, cols], preferred_element_type=F32)
-        g = g.reshape(16, 8, g.shape[1])
-        if half == 0:
-            first, second = g, pltpu.roll(g, 4, 1)
-        else:
-            first, second = halves(g[:, :, :half], g[:, :, half:])
-        for lo in range(2):
-            for x in range(4):
-                for core in range(2):
-                    put(core, x, lo, z, first[(lo * 4 + x) * 2 + core])
-                    put(core, x, 2 + lo, z, second[(lo * 4 + x) * 2 + core])
-        return carry
-
-    lax.fori_loop(0, 8, step, 0)
+def last_chunk(left, right, total, cols, put):
+    rows = slice((NCHUNK - 1) * CROWS, NCHUNK * CROWS)
+
+    def step(i, carry):
+        at = pl.ds(pl.multiple_of(i * 256, 256), 256)
+        g = total[at, cols] + jnp.dot(left[at, rows], right[rows, cols], preferred_element_type=F32)
+        g = g.reshape(2, 2, 4, 2, 8, g.shape[1])
+        for j in range(2):
+            put(i * 2 + j, g[j])
+        return carry
+
+    lax.fori_loop(0, 4, step, 0)
 
 
 def kernel(
-    lat_hbm, w_in_hbm, w_out_hbm, obs_hbm, idx_hbm, cnt_hbm, out1, out2,
+    lat_hbm, w_in_hbm, w_out_hbm, obs_hbm, idx_hbm, cnt_hbm, out,
     lat, w_in, w_raw, wo, wo_t, obs, idx, cnt, pre, hid, dec, x, tgt, target, own, weight, part, inv, ret, back,
-    go, gp, lat_t, hid_t, qa, qb, qc, a0, b0, c0, a1, b1, c1, a2, b2, c2, a3, b3, c3,
+    go, gp, lat_t, hid_t, sum1, sum2, qa, qb, qc, a0, b0, c0, a1, b1, c1, a2, b2, c2, a3, b3, c3,
     load_sem, there_send, there_recv, back_send, back_recv, rs_send, rs_recv,
 ):
     m, t, b = lax.axis_index("member"), lax.axis_index("tile"), lax.axis_index("batch")
@@ -163,22 +165,28 @@
     for o in (1, 2, 3):
         pl.semaphore_signal(barrier, inc=1, device_id=at_y(o), device_id_type=MESH)
 
-    loads = [pltpu.make_async_copy(w_in_hbm, w_in, load_sem.at[0])]
+    def load_lat(c):
+        rows = pl.ds(pl.multiple_of(c * CROWS, CROWS), CROWS)
+        return pltpu.make_async_copy(lat_hbm.at[0, 0, rows, :], lat.at[rows, :], load_sem.at[c])
+
+    load_w = pltpu.make_async_copy(w_in_hbm, w_in, load_sem.at[4])
+    load_wo = pltpu.make_async_copy(w_out_hbm, w_raw, load_sem.at[5])
+    later = [
+        pltpu.make_async_copy(obs_hbm.at[0], obs, load_sem.at[6]),
+        pltpu.make_async_copy(idx_hbm, idx, load_sem.at[7]),
+        pltpu.make_async_copy(cnt_hbm, cnt, load_sem.at[8]),
+    ]
+    load_wo.start()
+    load_w.start()
     for c in range(NCHUNK):
-        rows = pl.ds(c * CROWS, CROWS)
-        loads.append(pltpu.make_async_copy(lat_hbm.at[0, 0, rows, :], lat.at[rows, :], load_sem.at[1 + c]))
-    loads.append(pltpu.make_async_copy(w_out_hbm, w_raw, load_sem.at[5]))
-    loads.append(pltpu.make_async_copy(obs_hbm.at[0], obs, load_sem.at[6]))
-    loads.append(pltpu.make_async_copy(idx_hbm, idx, load_sem.at[7]))
-    loads.append(pltpu.make_async_copy(cnt_hbm, cnt, load_sem.at[8]))
-    for load in loads:
+        load_lat(c).start()
+    for load in later:
         load.start()
-    wo[...] = jnp.zeros(wo.shape, wo.dtype)
-    loads[5].wait()
-    wo[:, :CH] = w_raw[...]
-    for load in loads[:5]:
-        load.wait()
-    pl.semaphore_wait(barrier, len(peers) + 3)
+    wo_t[CH:, :] = jnp.zeros((LANE - CH, HID), BF16)
+    load_wo.wait()
+    wo_t[:CH, :] = w_raw[...]
+    wo[...] = wo_t[...].T
+    load_w.wait()
 
     def there(c, o):
         return pltpu.make_async_remote_copy(
@@ -194,34 +202,41 @@
             device_id=at_member(o), device_id_type=MESH,
         )
 
+    def arrived(make, c):
+        for o in range(1, MEMBERS):
+            make(c, o).wait_recv()
+
     def forward(c, carry):
+        load_lat(c).wait()
         forward_chunk(c, lat, w_in, wo, pre, hid, dec)
+        return carry
+
+    def depart(c):
         x[m, c] = dec[c, m]
         for o in ORDER:
             there(c, o).start()
-        return carry
-
-    lax.fori_loop(0, NCHUNK, forward, 0)
-
-    for load in loads[6:]:
+
+    def forward_and_depart(c, carry):
+        forward(c, carry)
+        depart(c)
+        return carry
+
+    forward(0, 0)
+    pl.semaphore_wait(barrier, len(peers) + 3)
+    depart(0)
+    lax.fori_loop(1, NCHUNK, forward_and_depart, 0)
+
+    for load in later:
         load.wait()
-    wo_t[...] = wo[...].T
     own_term(obs, idx, cnt, dec, tgt, target, own, weight)
     slopes(pre)
     transposed(hid, hid_t)
     transposed(lat, lat_t)
-
-    def arrived(make):
-        def step(c, carry):
-            for o in range(1, MEMBERS):
-                make(c, o).wait_recv()
-            return carry
-
-        return step
-
-    lax.fori_loop(0, NCHUNK, arrived(there), 0)
+    sum1[...] = jnp.zeros(sum1.shape, F32)
+    sum2[...] = jnp.zeros(sum2.shape, F32)
 
     def score(c, carry):
+        arrived(there, c)
         pair_patch(c, x, part, inv, ret)
         back[c, m] = ret[c, m]
         for o in ORDER:
@@ -231,11 +246,15 @@
     lax.fori_loop(0, NCHUNK, score, 0)
 
     def backward(c, carry):
-        arrived(returned)(c, 0)
+        arrived(returned, c)
         backward_chunk(c, back, own, weight, wo_t, pre, go, gp)
-        return carry
-
-    lax.fori_loop(0, NCHUNK, backward, 0)
+        accumulate(c, hid_t, go, sum2)
+        accumulate(c, lat_t, gp, sum1)
+        return carry
+
+    lax.fori_loop(0, NCHUNK - 1, backward, 0)
+    arrived(returned, NCHUNK - 1)
+    backward_chunk(NCHUNK - 1, back, own, weight, wo_t, pre, go, gp)
 
     slots = iter(range(45))
 
@@ -265,22 +284,36 @@
 
         lax.fori_loop(0, n, step, 0)
 
-    def put_a(k, x_, y_, z_, value):
-        qa[k, x_, y_, z_] = value
-
-    def put_b(k, x_, y_, z_, value):
-        qb[k, y_, x_, z_] = value
-
-    def put_c(k, x_, y_, z_, value):
-        qc[k, z_, x_, y_] = value
-
-    weight_grad(hid_t, go, slice(0, 128), 0, put_c)
+    def put_a(k, g):
+        first, second = halves(g[..., :256], g[..., 256:])
+        for lo in range(2):
+            for x_ in range(4):
+                for core_ in range(2):
+                    qa[core_, x_, lo, k] = first[lo, x_, core_]
+                    qa[core_, x_, 2 + lo, k] = second[lo, x_, core_]
+
+    def put_b(k, g):
+        first, second = halves(g[..., :256], g[..., 256:])
+        for lo in range(2):
+            for x_ in range(4):
+                for core_ in range(2):
+                    qb[core_, lo, x_, k] = first[lo, x_, core_]
+                    qb[core_, 2 + lo, x_, k] = second[lo, x_, core_]
+
+    def put_c(k, g):
+        first, second = halves(g[0], g[1])
+        for x_ in range(4):
+            for core_ in range(2):
+                qc[core_, k, x_, 0] = first[x_, core_]
+                qc[core_, k, x_, 1] = second[x_, core_]
+
+    last_chunk(hid_t, go, sum2, slice(0, LANE), put_c)
     c_core = send(qc.at[1 - core], c0.at[0], at_core())
-    weight_grad(lat_t, gp, slice(0, 512), 256, put_a)
+    last_chunk(lat_t, gp, sum1, slice(0, 512), put_a)
     a_core = send(qa.at[1 - core], a0.at[0], at_core())
     added(qc.at[core], c0, [c_core])
     c_one = [send(qc.at[core, (z + o) % 8], c1.at[o - 1], at_z(o)) for o in (4, 3, 5, 2, 6, 1, 7)]
-    weight_grad(lat_t, gp, slice(512, 1024), 256, put_b)
+    last_chunk(lat_t, gp, sum1, slice(512, 1024), put_b)
     b_core = send(qb.at[1 - core], b0.at[0], at_core())
     added(qa.at[core], a0, [a_core])
     a_one = [send(qa.at[core, (xx + o) % 4], a1.at[o - 1], at_x(o)) for o in (2, 1, 3)]
@@ -293,7 +326,7 @@
     added(qb.at[core, y], b1, b_one)
     b_two = [send(qb.at[core, y, (xx + o) % 4], b2.at[o - 1], at_x(o)) for o in (2, 1, 3)]
     added(qc.at[core, z, xx], c2, c_two)
-    c_three = [send(qc.at[core, z, xx, (y + o) % 4], c3.at[o - 1], at_y(o)) for o in (2, 1, 3)]
+    c_three = [send(qc.at[core, z, xx, (y + o) % 4 // 2], c3.at[o - 1], at_y(o)) for o in (2, 1, 3)]
     added(qa.at[core, xx, y], a2, a_two)
     a_three = [send(qa.at[core, xx, y, (z + o) % 8], a3.at[o - 1], at_z(o)) for o in (4, 3, 5, 2, 6, 1, 7)]
     added(qb.at[core, y, xx], b2, b_two)
@@ -306,14 +339,10 @@
             value = value + landed[j]
         return value
 
-    total = last(qc[core, z, xx, y], c3, c_three)
-    out2[...] = total[:4, :CH]
-    total = last(qa[core, xx, y, z], a3, a_three)
-    out1[:, 0:256] = total[:4]
-    out1[:, 256:512] = pltpu.roll(total, 4, 0)[:4]
-    total = last(qb[core, y, xx, z], b3, b_three)
-    out1[:, 512:768] = total[:4]
-    out1[:, 768:1024] = pltpu.roll(total, 4, 0)[:4]
+    total = last(qc[core, z, xx, b], c3, c_three)
+    out[:, 512:] = jnp.where(y_lo == 0, total, pltpu.roll(total, 4, 0))
+    out[:, :256] = last(qa[core, xx, y, z], a3, a_three)
+    out[:, 256:512] = last(qb[core, y, xx, z], b3, b_three)
 
     for copy in sent:
         copy.wait_send()
@@ -330,17 +359,18 @@
 def scratch():
     v = pltpu.VMEM
     return [
-        v((ROWS, D), BF16), v((D, HID), BF16), v((HID, CH), BF16), v((HID, LANE), BF16), v((LANE, HID), BF16),
+        v((ROWS, D), BF16), v((D, HID), BF16), v((CH, HID), BF16), v((HID, LANE), BF16), v((LANE, HID), BF16),
         v((POOL, FEAT), BF16), v((1, NPATCH), jnp.int32), v((1, NPATCH), jnp.int32),
         v((ROWS, HID), F32), v((ROWS, HID), BF16), v((NCHUNK, MEMBERS, PATCH, LANE), F32),
         v((MEMBERS, NCHUNK, PATCH, LANE), F32), v((NPATCH, FEAT), BF16), v((ROWS, LANE), F32),
         v((ROWS, LANE), F32), v((ROWS, LANE), F32), v((len(PAIRS), 8, LANE), F32), v((len(PAIRS), LANE), F32),
         v((NCHUNK, MEMBERS, PATCH, LANE), F32), v((NCHUNK, MEMBERS, PATCH, LANE), F32),
         v((ROWS, LANE), BF16), v((ROWS, HID), BF16), v((D, ROWS), BF16), v((HID, ROWS), BF16),
-        v((2, 4, 4, 8, 8, 256), F32), v((2, 4, 4, 8, 8, 256), F32), v((2, 8, 4, 4, 8, 128), F32),
-        v((1, 4, 4, 8, 8, 256), F32), v((1, 4, 4, 8, 8, 256), F32), v((1, 8, 4, 4, 8, 128), F32),
-        v((3, 4, 8, 8, 256), F32), v((3, 4, 8, 8, 256), F32), v((7, 4, 4, 8, 128), F32),
-        v((3, 8, 8, 256), F32), v((3, 8, 8, 256), F32), v((3, 4, 8, 128), F32),
+        v((D, HID), F32), v((HID, LANE), F32),
+        v((2, 4, 4, 8, 8, 256), F32), v((2, 4, 4, 8, 8, 256), F32), v((2, 8, 4, 2, 8, 128), F32),
+        v((1, 4, 4, 8, 8, 256), F32), v((1, 4, 4, 8, 8, 256), F32), v((1, 8, 4, 2, 8, 128), F32),
+        v((3, 4, 8, 8, 256), F32), v((3, 4, 8, 8, 256), F32), v((7, 4, 2, 8, 128), F32),
+        v((3, 8, 8, 256), F32), v((3, 8, 8, 256), F32), v((3, 2, 8, 128), F32),
         v((7, 8, 256), F32), v((7, 8, 256), F32), v((3, 8, 128), F32),
         pltpu.SemaphoreType.DMA((9,)),
         pltpu.SemaphoreType.DMA((NCHUNK, MEMBERS)), pltpu.SemaphoreType.DMA((NCHUNK, MEMBERS)),
@@ -349,17 +379,29 @@
     ]
 
 
+def unpack(packed, out1, out2):
+    for i in range(2):
+        value = packed[:, i * 256 : i * 256 + 256]
+        out1[:, i * 512 : i * 512 + 256] = value[:4]
+        out1[:, i * 512 + 256 : i * 512 + 512] = pltpu.roll(value, 4, 0)[:4]
+    out2[...] = packed[:4, 512 : 512 + CH]
+
+
 def shards(latent, w_in, w_out, observed, patch_index, counts):
-    return pl.pallas_call(
+    packed = pl.pallas_call(
         kernel,
-        out_shape=(jax.ShapeDtypeStruct((4, HID), F32), jax.ShapeDtypeStruct((4, CH), F32)),
+        out_shape=jax.ShapeDtypeStruct((8, 640), F32),
         in_specs=[pl.BlockSpec(memory_space=pl.ANY)] * 6,
-        out_specs=(pl.BlockSpec(memory_space=pltpu.VMEM), pl.BlockSpec(memory_space=pltpu.VMEM)),
+        out_specs=pl.BlockSpec(memory_space=pltpu.VMEM),
         scratch_shapes=scratch(),
         compiler_params=pltpu.CompilerParams(
             collective_id=0, has_side_effects=True, vmem_limit_bytes=60 * 1024 * 1024
         ),
-    )(latent, w_in, w_out, observed, patch_index, counts)
+    )(latent, w_in, w_out.T, observed, patch_index, counts)
+    return pl.pallas_call(
+        unpack,
+        out_shape=(jax.ShapeDtypeStruct((4, HID), F32), jax.ShapeDtypeStruct((4, CH), F32)),
+    )(packed)
 
 
 def solution(mesh):

time: 81.7 us -> 72.4 us (0.89)
  Pallas kernels: 76.5 us -> 71.6 us
  local copies, waits for them, and re-layouts: 4.35 us -> 0 us
    pallas_call x1 -> x2, Pallas kernels: 76.5 us -> 71.6 us  [the longest x1 70.2 us: shards(): pl.pallas_call(kernel, out_shape=jax.ShapeDtypeStruct((8, 640), F32), in_...]
    unnamed x3 -> x0, local copies, waits for them, and re-layouts: 4.35 us -> none
where the time goes in v2:
time: 72.4 us; the launch traced here: 72.2 us
  Pallas kernels  71.6 us (99%)
    pallas_call x1, Pallas kernels, shards(): pl.pallas_call(kernel, out_shape=jax.ShapeDtypeStruct((8, 640), F32), in_...  70.2 us

profile of v2, /device:TPU:1, one launch (start us, length us, event | category | flops | bytes accessed | tf_op | source)
XLA Modules:
  0.0 72.2 jit_solution(12372054609389854391)
XLA Ops:
  0.6 70.2 %shard_map.77.packed = f32[8,640]{1,0:T(8,128)} custom-call(bf16[1,1,1024,1024]{3,2,1,0:T(8,128)(2,1)} %lat_hbm.1, bf16[1024,1024]{1,0:T(8,128)(2,1)} %w_in_hbm.1, bf16[112,1024]{1,0:T(8,128)(2,1)} %bitcast.1, bf16[1,128,1792]{2,1,0:T(8,128)(2,1)} %obs_hbm.1, s32[1,64]{1,0:T(1,128)} %idx_hbm.1, s32[1,64]{1,0:T(1,128)} %cnt_hbm.1), custom_call_target="tpu_custom_call" | custom-call | tf_op jit(solution)/shard_map/pallas_call | solution.py:391
  70.9 1.3 %shard_map.78 = (f32[4,1024]{1,0:T(4,128)}, f32[4,112]{1,0:T(4,128)}) custom-call(f32[8,640]{1,0:T(8,128)} %shard_map.77.packed), custom_call_target="tpu_custom_call" | custom-call | tf_op jit(solution)/shard_map/pallas_call | solution.py:401

commit v3 on v2

--- a/solution.py
+++ b/solution.py
@@ -10,6 +10,7 @@
 ROWS, D, HID, CH, LANE = 1024, 1024, 1024, 112, 128
 PATCH, NPATCH, MEMBERS, POOL, FEAT = 16, 64, 16, 128, 1792
 NCHUNK, CROWS = 4, 256
+SLOTS = 96
 ORDER = (1, 15, 2, 14, 3, 13, 4, 12, 5, 11, 6, 10, 7, 9, 8)
 PAIRS = [(i, k) for i in range(MEMBERS) for k in range(i + 1, MEMBERS)]
 PAIR_AT = {pair: at for at, pair in enumerate(PAIRS)}
@@ -118,24 +119,18 @@
     return jnp.where(top, lo, pltpu.roll(hi, 4, axis)), jnp.where(top, pltpu.roll(lo, 4, axis), hi)
 
 
-def last_chunk(left, right, total, cols, put):
+def last_chunk(left, right, total, i):
     rows = slice((NCHUNK - 1) * CROWS, NCHUNK * CROWS)
-
-    def step(i, carry):
-        at = pl.ds(pl.multiple_of(i * 256, 256), 256)
-        g = total[at, cols] + jnp.dot(left[at, rows], right[rows, cols], preferred_element_type=F32)
-        g = g.reshape(2, 2, 4, 2, 8, g.shape[1])
-        for j in range(2):
-            put(i * 2 + j, g[j])
-        return carry
-
-    lax.fori_loop(0, 4, step, 0)
+    at = slice(i * 256, i * 256 + 256)
+    g = total[at, :] + jnp.dot(left[at, rows], right[rows, :], preferred_element_type=F32)
+    return g.reshape(2, 2, 4, 2, 8, g.shape[1])
 
 
 def kernel(
     lat_hbm, w_in_hbm, w_out_hbm, obs_hbm, idx_hbm, cnt_hbm, out,
     lat, w_in, w_raw, wo, wo_t, obs, idx, cnt, pre, hid, dec, x, tgt, target, own, weight, part, inv, ret, back,
-    go, gp, lat_t, hid_t, sum1, sum2, qa, qb, qc, a0, b0, c0, a1, b1, c1, a2, b2, c2, a3, b3, c3,
+    go, gp, lat_t, hid_t, sum1, sum2, qa, qb, qc,
+    a0, b0, c0, ah, bh, c1, an, bn, af, bf, a2, b2, c2, a3, b3, c3,
     load_sem, there_send, there_recv, back_send, back_recv, rs_send, rs_recv,
 ):
     m, t, b = lax.axis_index("member"), lax.axis_index("tile"), lax.axis_index("batch")
@@ -256,7 +251,8 @@
     arrived(returned, NCHUNK - 1)
     backward_chunk(NCHUNK - 1, back, own, weight, wo_t, pre, go, gp)
 
-    slots = iter(range(45))
+    slots = iter(range(SLOTS))
+    sent = []
 
     def send(src, dst, device):
         at = next(slots)
@@ -268,69 +264,70 @@
         sent.append(copy)
         return copy
 
-    sent = []
-
     def added(own_ref, landed, copies):
         for copy in copies:
             copy.wait_recv()
-        n = own_ref.shape[0]
-
-        def step(i, carry):
-            total = own_ref[i]
-            for j in range(landed.shape[0]):
-                total = total + landed[j, i]
-            own_ref[i] = total
-            return carry
-
-        lax.fori_loop(0, n, step, 0)
-
-    def put_a(k, g):
-        first, second = halves(g[..., :256], g[..., 256:])
-        for lo in range(2):
-            for x_ in range(4):
-                for core_ in range(2):
-                    qa[core_, x_, lo, k] = first[lo, x_, core_]
-                    qa[core_, x_, 2 + lo, k] = second[lo, x_, core_]
-
-    def put_b(k, g):
-        first, second = halves(g[..., :256], g[..., 256:])
-        for lo in range(2):
-            for x_ in range(4):
-                for core_ in range(2):
-                    qb[core_, lo, x_, k] = first[lo, x_, core_]
-                    qb[core_, 2 + lo, x_, k] = second[lo, x_, core_]
-
-    def put_c(k, g):
-        first, second = halves(g[0], g[1])
-        for x_ in range(4):
-            for core_ in range(2):
-                qc[core_, k, x_, 0] = first[x_, core_]
-                qc[core_, k, x_, 1] = second[x_, core_]
-
-    last_chunk(hid_t, go, sum2, slice(0, LANE), put_c)
-    c_core = send(qc.at[1 - core], c0.at[0], at_core())
-    last_chunk(lat_t, gp, sum1, slice(0, 512), put_a)
-    a_core = send(qa.at[1 - core], a0.at[0], at_core())
-    added(qc.at[core], c0, [c_core])
-    c_one = [send(qc.at[core, (z + o) % 8], c1.at[o - 1], at_z(o)) for o in (4, 3, 5, 2, 6, 1, 7)]
-    last_chunk(lat_t, gp, sum1, slice(512, 1024), put_b)
-    b_core = send(qb.at[1 - core], b0.at[0], at_core())
-    added(qa.at[core], a0, [a_core])
-    a_one = [send(qa.at[core, (xx + o) % 4], a1.at[o - 1], at_x(o)) for o in (2, 1, 3)]
-    added(qb.at[core], b0, [b_core])
-    b_one = [send(qb.at[core, (y + o) % 4], b1.at[o - 1], at_y(o)) for o in (2, 1, 3)]
-    added(qc.at[core, z], c1, c_one)
-    c_two = [send(qc.at[core, z, (xx + o) % 4], c2.at[o - 1], at_x(o)) for o in (2, 1, 3)]
-    added(qa.at[core, xx], a1, a_one)
-    a_two = [send(qa.at[core, xx, (y + o) % 4], a2.at[o - 1], at_y(o)) for o in (2, 1, 3)]
-    added(qb.at[core, y], b1, b_one)
-    b_two = [send(qb.at[core, y, (xx + o) % 4], b2.at[o - 1], at_x(o)) for o in (2, 1, 3)]
-    added(qc.at[core, z, xx], c2, c_two)
-    c_three = [send(qc.at[core, z, xx, (y + o) % 4 // 2], c3.at[o - 1], at_y(o)) for o in (2, 1, 3)]
-    added(qa.at[core, xx, y], a2, a_two)
-    a_three = [send(qa.at[core, xx, y, (z + o) % 8], a3.at[o - 1], at_z(o)) for o in (4, 3, 5, 2, 6, 1, 7)]
-    added(qb.at[core, y, xx], b2, b_two)
-    b_three = [send(qb.at[core, y, xx, (z + o) % 8], b3.at[o - 1], at_z(o)) for o in (4, 3, 5, 2, 6, 1, 7)]
+        total = own_ref[...]
+        for ref in landed:
+            total = total + ref[...]
+        own_ref[...] = total
+
+    class Group:
+        def __init__(self, q, core_in, hop_in, near_in, far_in, second_in, third_in, at_p, at_q, p, q_at):
+            self.q, self.core_in, self.hop_in, self.near_in, self.far_in = q, core_in, hop_in, near_in, far_in
+            self.second_in, self.third_in, self.at_p, self.at_q = second_in, third_in, at_p, at_q
+            self.p, self.q_at = p, q_at
+            self.core_copy, self.hop, self.near, self.far, self.second = {}, {}, {}, {}, {}
+
+        def part(self, to, h, k):
+            return self.q.at[core, to, pl.ds(2 * h, 2), pl.ds(2 * k, 2)]
+
+        def exchange(self, k):
+            self.core_copy[k] = send(
+                self.q.at[1 - core, :, :, pl.ds(2 * k, 2)], self.core_in.at[k], at_core()
+            )
+
+        def first(self, k):
+            added(self.q.at[core, :, :, pl.ds(2 * k, 2)], [self.core_in.at[k]], [self.core_copy[k]])
+            for h, s in ((0, 1), (1, 3)):
+                self.hop[k, h] = send(self.part((self.p + 2) % 4, h, k), self.hop_in.at[k, h], self.at_p(s))
+            for h, s in ((0, 1), (1, 3)):
+                back_to = 4 - s
+                self.near[k, h] = send(
+                    self.part((self.p + back_to) % 4, h, k), self.near_in.at[k, h], self.at_p(back_to)
+                )
+
+        def relay(self, k):
+            for h, s in ((0, 1), (1, 3)):
+                added(self.hop_in.at[k, h], [self.part((self.p + s) % 4, h, k)], [self.hop[k, h]])
+                self.far[k, h] = send(self.hop_in.at[k, h], self.far_in.at[k, h], self.at_p(s))
+
+        def finish(self, k):
+            for h in range(2):
+                added(
+                    self.part(self.p, h, k), [self.near_in.at[k, h], self.far_in.at[k, h]],
+                    [self.near[k, h], self.far[k, h]],
+                )
+
+        def other_ring(self, i):
+            zs = pl.ds(4 * i, 4)
+            self.second[i] = [
+                send(self.q.at[core, self.p, (self.q_at + o) % 4, zs], self.second_in.at[i, o - 1], self.at_q(o))
+                for o in (2, 1, 3)
+            ]
+
+        def collect(self, i):
+            landed = [self.second_in.at[i, o] for o in range(3)]
+            added(self.q.at[core, self.p, self.q_at, pl.ds(4 * i, 4)], landed, self.second[i])
+
+        def along_z(self):
+            self.third = [
+                send(self.q.at[core, self.p, self.q_at, (z + o) % 8], self.third_in.at[o - 1], at_z(o))
+                for o in (4, 3, 5, 2, 6, 1, 7)
+            ]
+
+        def result(self):
+            return last(self.q[core, self.p, self.q_at, z], self.third_in, self.third)
 
     def last(value, landed, copies):
         for copy in copies:
@@ -339,10 +336,70 @@
             value = value + landed[j]
         return value
 
+    ga = Group(qa, a0, ah, an, af, a2, a3, at_x, at_y, xx, y)
+    gb = Group(qb, b0, bh, bn, bf, b2, b3, at_y, at_x, y, xx)
+    both = (ga, gb)
+
+    def product(k):
+        g = last_chunk(lat_t, gp, sum1, k)
+        for j in range(2):
+            a_lo, a_hi = halves(g[j, ..., :256], g[j, ..., 256:512])
+            b_lo, b_hi = halves(g[j, ..., 512:768], g[j, ..., 768:])
+            for lo in range(2):
+                for x_ in range(4):
+                    for core_ in range(2):
+                        qa[core_, x_, lo, 2 * k + j] = a_lo[lo, x_, core_]
+                        qa[core_, x_, 2 + lo, 2 * k + j] = a_hi[lo, x_, core_]
+                        qb[core_, lo, x_, 2 * k + j] = b_lo[lo, x_, core_]
+                        qb[core_, 2 + lo, x_, 2 * k + j] = b_hi[lo, x_, core_]
+        for group in both:
+            group.exchange(k)
+
+    def each(name, i):
+        for group in both:
+            getattr(group, name)(i)
+
+    for k in range(4):
+        g = last_chunk(hid_t, go, sum2, k)
+        for j in range(2):
+            c_lo, c_hi = halves(g[j, 0], g[j, 1])
+            for x_ in range(4):
+                for core_ in range(2):
+                    qc[core_, 2 * k + j, x_, 0] = c_lo[x_, core_]
+                    qc[core_, 2 * k + j, x_, 1] = c_hi[x_, core_]
+    c_core = send(qc.at[1 - core], c0, at_core())
+    product(0)
+    product(1)
+    added(qc.at[core], [c0], [c_core])
+    c_one = [send(qc.at[core, (z + o) % 8], c1.at[o - 1], at_z(o)) for o in (4, 3, 5, 2, 6, 1, 7)]
+    each("first", 0)
+    product(2)
+    each("first", 1)
+    product(3)
+    each("relay", 0)
+    each("first", 2)
+    each("relay", 1)
+    each("first", 3)
+    each("relay", 2)
+    each("relay", 3)
+    each("finish", 0)
+    each("finish", 1)
+    each("other_ring", 0)
+    added(qc.at[core, z], [c1.at[j] for j in range(7)], c_one)
+    c_two = [send(qc.at[core, z, (xx + o) % 4], c2.at[o - 1], at_x(o)) for o in (2, 1, 3)]
+    each("finish", 2)
+    each("finish", 3)
+    each("other_ring", 1)
+    added(qc.at[core, z, xx], [c2.at[j] for j in range(3)], c_two)
+    c_three = [send(qc.at[core, z, xx, (y + o) % 4 // 2], c3.at[o - 1], at_y(o)) for o in (2, 1, 3)]
+    each("collect", 0)
+    each("collect", 1)
+    for group in both:
+        group.along_z()
     total = last(qc[core, z, xx, b], c3, c_three)
     out[:, 512:] = jnp.where(y_lo == 0, total, pltpu.roll(total, 4, 0))
-    out[:, :256] = last(qa[core, xx, y, z], a3, a_three)
-    out[:, 256:512] = last(qb[core, y, xx, z], b3, b_three)
+    out[:, :256] = ga.result()
+    out[:, 256:512] = gb.result()
 
     for copy in sent:
         copy.wait_send()
@@ -368,14 +425,16 @@
         v((ROWS, LANE), BF16), v((ROWS, HID), BF16), v((D, ROWS), BF16), v((HID, ROWS), BF16),
         v((D, HID), F32), v((HID, LANE), F32),
         v((2, 4, 4, 8, 8, 256), F32), v((2, 4, 4, 8, 8, 256), F32), v((2, 8, 4, 2, 8, 128), F32),
-        v((1, 4, 4, 8, 8, 256), F32), v((1, 4, 4, 8, 8, 256), F32), v((1, 8, 4, 2, 8, 128), F32),
-        v((3, 4, 8, 8, 256), F32), v((3, 4, 8, 8, 256), F32), v((7, 4, 2, 8, 128), F32),
-        v((3, 8, 8, 256), F32), v((3, 8, 8, 256), F32), v((3, 2, 8, 128), F32),
+        v((4, 4, 4, 2, 8, 256), F32), v((4, 4, 4, 2, 8, 256), F32), v((8, 4, 2, 8, 128), F32),
+        v((4, 2, 2, 2, 8, 256), F32), v((4, 2, 2, 2, 8, 256), F32), v((7, 4, 2, 8, 128), F32),
+        v((4, 2, 2, 2, 8, 256), F32), v((4, 2, 2, 2, 8, 256), F32),
+        v((4, 2, 2, 2, 8, 256), F32), v((4, 2, 2, 2, 8, 256), F32),
+        v((2, 3, 4, 8, 256), F32), v((2, 3, 4, 8, 256), F32), v((3, 2, 8, 128), F32),
         v((7, 8, 256), F32), v((7, 8, 256), F32), v((3, 8, 128), F32),
         pltpu.SemaphoreType.DMA((9,)),
         pltpu.SemaphoreType.DMA((NCHUNK, MEMBERS)), pltpu.SemaphoreType.DMA((NCHUNK, MEMBERS)),
         pltpu.SemaphoreType.DMA((NCHUNK, MEMBERS)), pltpu.SemaphoreType.DMA((NCHUNK, MEMBERS)),
-        pltpu.SemaphoreType.DMA((45,)), pltpu.SemaphoreType.DMA((45,)),
+        pltpu.SemaphoreType.DMA((SLOTS,)), pltpu.SemaphoreType.DMA((SLOTS,)),
     ]
 
 

time: 72.4 us -> 68.4 us (0.945)
  Pallas kernels: 71.6 us -> 67.6 us
    pallas_call x1, Pallas kernels: 70.2 us -> 66.3 us  [shards(): pl.pallas_call(kernel, out_shape=jax.ShapeDtypeStruct((8, 640), F32), in_...]
where the time goes in v3:
time: 68.4 us; the launch traced here: 68.3 us
  Pallas kernels  67.6 us (99%)
    pallas_call x1, Pallas kernels, shards(): pl.pallas_call(kernel, out_shape=jax.ShapeDtypeStruct((8, 640), F32), in_...  66.3 us

profile of v3, /device:TPU:1, one launch (start us, length us, event | category | flops | bytes accessed | tf_op | source)
XLA Modules:
  0.0 68.3 jit_solution(15766853970031612635)
XLA Ops:
  0.6 66.3 %shard_map.77.packed = f32[8,640]{1,0:T(8,128)} custom-call(bf16[1,1,1024,1024]{3,2,1,0:T(8,128)(2,1)} %lat_hbm.1, bf16[1024,1024]{1,0:T(8,128)(2,1)} %w_in_hbm.1, bf16[112,1024]{1,0:T(8,128)(2,1)} %bitcast.1, bf16[1,128,1792]{2,1,0:T(8,128)(2,1)} %obs_hbm.1, s32[1,64]{1,0:T(1,128)} %idx_hbm.1, s32[1,64]{1,0:T(1,128)} %cnt_hbm.1), custom_call_target="tpu_custom_call" | custom-call | tf_op jit(solution)/shard_map/pallas_call | solution.py:450
  66.9 1.3 %shard_map.78 = (f32[4,1024]{1,0:T(4,128)}, f32[4,112]{1,0:T(4,128)}) custom-call(f32[8,640]{1,0:T(8,128)} %shard_map.77.packed), custom_call_target="tpu_custom_call" | custom-call | tf_op jit(solution)/shard_map/pallas_call | solution.py:460

commit v4 on v3

--- a/solution.py
+++ b/solution.py
@@ -11,18 +11,46 @@
 PATCH, NPATCH, MEMBERS, POOL, FEAT = 16, 64, 16, 128, 1792
 NCHUNK, CROWS = 4, 256
 SLOTS = 96
+VMEM_KIB = 55100
+SENT = 14
 ORDER = (1, 15, 2, 14, 3, 13, 4, 12, 5, 11, 6, 10, 7, 9, 8)
 PAIRS = [(i, k) for i in range(MEMBERS) for k in range(i + 1, MEMBERS)]
 PAIR_AT = {pair: at for at, pair in enumerate(PAIRS)}
 
 
-def forward_chunk(c, lat, w_in, wo, pre, hid, dec):
+def row_and_lane(shape):
+    return lax.broadcasted_iota(jnp.int32, shape, 0), lax.broadcasted_iota(jnp.int32, shape, 1)
+
+
+def pack_patch(value):
+    row, lane = row_and_lane((PATCH, LANE))
+    low = jnp.broadcast_to(value[14:15], (PATCH, LANE))
+    high = pltpu.roll(jnp.broadcast_to(value[15:16], (PATCH, LANE)), 16, 1)
+    moved = pltpu.roll(jnp.where(row < 7, low, high), 16, 1, stride=16, stride_axis=0)
+    return jnp.where(row < SENT, jnp.where(lane < CH, value, moved), 0.0)
+
+
+def unpack_patch(value):
+    row, lane = row_and_lane((PATCH, LANE))
+    moved = jnp.where((lane >= CH) & (row < SENT), value, 0.0)
+    groups = jnp.where(row < 7, 7 - row, 14 - row)
+    for bit in (4, 2, 1):
+        moved = jnp.where((groups & bit) != 0, pltpu.roll(moved, 16 * bit, 1), moved)
+    low = jnp.sum(jnp.where(row < 7, moved, 0.0), axis=0, keepdims=True)
+    high = jnp.sum(jnp.where(row < 7, 0.0, moved), axis=0, keepdims=True)
+    tail = jnp.where(row == 14, low, high)
+    return jnp.where(row < SENT, jnp.where(lane < CH, value, 0.0), tail)
+
+
+def forward_chunk(c, lat, w_in, wo, pre, hid, dec, packed):
     rows = pl.ds(pl.multiple_of(c * CROWS, CROWS), CROWS)
     v = jnp.dot(lat[rows, :], w_in[...], preferred_element_type=F32)
     pre[rows, :] = v
     hid[rows, :] = (v * (1.0 / (1.0 + jnp.exp(-v)))).astype(BF16)
     out = jnp.dot(hid[rows, :], wo[...], preferred_element_type=F32)
     dec[c] = out.reshape(MEMBERS, PATCH, LANE)
+    for j in range(MEMBERS):
+        packed[c, j] = pack_patch(out[j * PATCH : j * PATCH + PATCH])
 
 
 def slopes(pre):
@@ -95,7 +123,7 @@
 
 def backward_chunk(c, back, own, weight, wo_t, slope, go, gp):
     rows = pl.ds(pl.multiple_of(c * CROWS, CROWS), CROWS)
-    pair = back[c].reshape(CROWS, LANE)
+    pair = jnp.concatenate([unpack_patch(back[c, j]) for j in range(MEMBERS)], axis=0)
     grad = (own[rows, :] - weight[rows, :] * pair).astype(BF16)
     go[rows, :] = grad
     gh = jnp.dot(grad, wo_t[...], preferred_element_type=F32)
@@ -128,7 +156,7 @@
 
 def kernel(
     lat_hbm, w_in_hbm, w_out_hbm, obs_hbm, idx_hbm, cnt_hbm, out,
-    lat, w_in, w_raw, wo, wo_t, obs, idx, cnt, pre, hid, dec, x, tgt, target, own, weight, part, inv, ret, back,
+    lat, w_in, w_raw, wo, wo_t, obs, idx, cnt, pre, hid, dec, packed, x, tgt, target, own, weight, part, inv, ret, back,
     go, gp, lat_t, hid_t, sum1, sum2, qa, qb, qc,
     a0, b0, c0, ah, bh, c1, an, bn, af, bf, a2, b2, c2, a3, b3, c3,
     load_sem, there_send, there_recv, back_send, back_recv, rs_send, rs_recv,
@@ -153,6 +181,7 @@
     def at_core():
         return {"tile": xx * 2 + (1 - core)}
 
+    x[...] = jnp.zeros(x.shape, F32)
     barrier = pltpu.get_barrier_semaphore()
     peers = [at_member(o) for o in range(1, 16)] + [at_core()] + [at_x(o) for o in range(1, 4)]
     for peer in peers:
@@ -185,14 +214,14 @@
 
     def there(c, o):
         return pltpu.make_async_remote_copy(
-            src_ref=dec.at[c, (m + o) % MEMBERS], dst_ref=x.at[m, c],
+            src_ref=packed.at[c, (m + o) % MEMBERS, pl.ds(0, SENT)], dst_ref=x.at[m, c, pl.ds(0, SENT)],
             send_sem=there_send.at[c, o], recv_sem=there_recv.at[c, o],
             device_id=at_member(o), device_id_type=MESH,
         )
 
     def returned(c, o):
         return pltpu.make_async_remote_copy(
-            src_ref=ret.at[c, (m + o) % MEMBERS], dst_ref=back.at[c, m],
+            src_ref=ret.at[c, (m + o) % MEMBERS, pl.ds(0, SENT)], dst_ref=back.at[c, m, pl.ds(0, SENT)],
             send_sem=back_send.at[c, o], recv_sem=back_recv.at[c, o],
             device_id=at_member(o), device_id_type=MESH,
         )
@@ -203,11 +232,11 @@
 
     def forward(c, carry):
         load_lat(c).wait()
-        forward_chunk(c, lat, w_in, wo, pre, hid, dec)
+        forward_chunk(c, lat, w_in, wo, pre, hid, dec, packed)
         return carry
 
     def depart(c):
-        x[m, c] = dec[c, m]
+        x[m, c] = packed[c, m]
         for o in ORDER:
             there(c, o).start()
 
@@ -418,7 +447,7 @@
     return [
         v((ROWS, D), BF16), v((D, HID), BF16), v((CH, HID), BF16), v((HID, LANE), BF16), v((LANE, HID), BF16),
         v((POOL, FEAT), BF16), v((1, NPATCH), jnp.int32), v((1, NPATCH), jnp.int32),
-        v((ROWS, HID), F32), v((ROWS, HID), BF16), v((NCHUNK, MEMBERS, PATCH, LANE), F32),
+        v((ROWS, HID), F32), v((ROWS, HID), BF16), v((NCHUNK, MEMBERS, PATCH, LANE), F32), v((NCHUNK, MEMBERS, PATCH, LANE), F32),
         v((MEMBERS, NCHUNK, PATCH, LANE), F32), v((NPATCH, FEAT), BF16), v((ROWS, LANE), F32),
         v((ROWS, LANE), F32), v((ROWS, LANE), F32), v((len(PAIRS), 8, LANE), F32), v((len(PAIRS), LANE), F32),
         v((NCHUNK, MEMBERS, PATCH, LANE), F32), v((NCHUNK, MEMBERS, PATCH, LANE), F32),
@@ -454,12 +483,13 @@
         out_specs=pl.BlockSpec(memory_space=pltpu.VMEM),
         scratch_shapes=scratch(),
         compiler_params=pltpu.CompilerParams(
-            collective_id=0, has_side_effects=True, vmem_limit_bytes=60 * 1024 * 1024
+            collective_id=0, has_side_effects=True, vmem_limit_bytes=VMEM_KIB * 1024
         ),
     )(latent, w_in, w_out.T, observed, patch_index, counts)
     return pl.pallas_call(
         unpack,
         out_shape=(jax.ShapeDtypeStruct((4, HID), F32), jax.ShapeDtypeStruct((4, CH), F32)),
+        compiler_params=pltpu.CompilerParams(vmem_limit_bytes=1024 * 1024),
     )(packed)
 
 

time: 68.4 us -> 66.3 us (0.969)
  Pallas kernels: 67.6 us -> 64.2 us
  local copies, waits for them, and re-layouts: 0 us -> 1.3 us
    pallas_call x1, Pallas kernels: 66.3 us -> 63.6 us  [shards(): pl.pallas_call(kernel, out_shape=jax.ShapeDtypeStruct((8, 640), F32), in_...]
    unnamed x0 -> x4, local copies, waits for them, and re-layouts: none -> 1.3 us
    pallas_call x1, Pallas kernels: 1.34 us -> 0.61 us  [shards(): pl.pallas_call(unpack, out_shape=(jax.ShapeDtypeStruct((4, HID), F32), ja...]
where the time goes in v4:
time: 66.3 us; the launch traced here: 66.2 us
  Pallas kernels  64.2 us (97%)
  local copies, waits for them, and re-layouts  1.3 us (2%)
    pallas_call x1, Pallas kernels, shards(): pl.pallas_call(kernel, out_shape=jax.ShapeDtypeStruct((8, 640), F32), in_...  63.6 us

profile of v4, /device:TPU:1, one launch (start us, length us, event | category | flops | bytes accessed | tf_op | source)
XLA Modules:
  0.0 66.2 jit_solution(5084820486172212842)
XLA Ops:
  0.6 0.0 copy-start
  0.6 0.6 copy-done
  1.3 0.0 copy-start.1
  1.3 0.7 copy-done.1
  1.9 63.6 %shard_map.77.packed = f32[8,640]{1,0:T(8,128)S(1)} custom-call(bf16[1,1,1024,1024]{3,2,1,0:T(8,128)(2,1)} %lat_hbm.1, bf16[1024,1024]{1,0:T(8,128)(2,1)} %w_in_hbm.1, bf16[112,1024]{1,0:T(8,128)(2,1)} %bitcast.1, bf16[1,128,1792]{2,1,0:T(8,128)(2,1)} %obs_hbm.1, s32[1,64]{1,0:T(1,128)S(1)} %copy-done, s32[1,64]{1,0:T(1,128)S(1)} %copy-done.1), custom_call_target="tpu_custom_call" | custom-call | tf_op jit(solution)/shard_map/pallas_call | solution.py:479
  65.5 0.6 shard_map.78
Async XLA Ops:
  0.6 0.7 copy-start
  1.3 0.7 copy-start.1

commit v5 on v4

--- a/solution.py
+++ b/solution.py
@@ -10,10 +10,10 @@
 ROWS, D, HID, CH, LANE = 1024, 1024, 1024, 112, 128
 PATCH, NPATCH, MEMBERS, POOL, FEAT = 16, 64, 16, 128, 1792
 NCHUNK, CROWS = 4, 256
-SLOTS = 96
+SLOTS = 82
 VMEM_KIB = 55100
 SENT = 14
-ORDER = (1, 15, 2, 14, 3, 13, 4, 12, 5, 11, 6, 10, 7, 9, 8)
+ORDER = (8, 7, 9, 6, 10, 5, 11, 4, 12, 3, 13, 2, 14, 1, 15)
 PAIRS = [(i, k) for i in range(MEMBERS) for k in range(i + 1, MEMBERS)]
 PAIR_AT = {pair: at for at, pair in enumerate(PAIRS)}
 
@@ -159,7 +159,7 @@
     lat, w_in, w_raw, wo, wo_t, obs, idx, cnt, pre, hid, dec, packed, x, tgt, target, own, weight, part, inv, ret, back,
     go, gp, lat_t, hid_t, sum1, sum2, qa, qb, qc,
     a0, b0, c0, ah, bh, c1, an, bn, af, bf, a2, b2, c2, a3, b3, c3,
-    load_sem, there_send, there_recv, back_send, back_recv, rs_send, rs_recv,
+    load_sem, there_send, there_recv, back_send, back_recv, rs_send, rs_recv, za_send, za_recv, zb_send, zb_recv,
 ):
     m, t, b = lax.axis_index("member"), lax.axis_index("tile"), lax.axis_index("batch")
     z, y_lo, xx, core = m // 2, m % 2, t // 2, t % 2
@@ -302,10 +302,10 @@
         own_ref[...] = total
 
     class Group:
-        def __init__(self, q, core_in, hop_in, near_in, far_in, second_in, third_in, at_p, at_q, p, q_at):
+        def __init__(self, q, core_in, hop_in, near_in, far_in, second_in, third_in, at_p, at_q, p, q_at, z_send, z_recv):
             self.q, self.core_in, self.hop_in, self.near_in, self.far_in = q, core_in, hop_in, near_in, far_in
             self.second_in, self.third_in, self.at_p, self.at_q = second_in, third_in, at_p, at_q
-            self.p, self.q_at = p, q_at
+            self.p, self.q_at, self.z_send, self.z_recv = p, q_at, z_send, z_recv
             self.core_copy, self.hop, self.near, self.far, self.second = {}, {}, {}, {}, {}
 
         def part(self, to, h, k):
@@ -349,14 +349,26 @@
             landed = [self.second_in.at[i, o] for o in range(3)]
             added(self.q.at[core, self.p, self.q_at, pl.ds(4 * i, 4)], landed, self.second[i])
 
-        def along_z(self):
-            self.third = [
-                send(self.q.at[core, self.p, self.q_at, (z + o) % 8], self.third_in.at[o - 1], at_z(o))
-                for o in (4, 3, 5, 2, 6, 1, 7)
-            ]
+        def to_z(self, o):
+            return pltpu.make_async_remote_copy(
+                src_ref=self.q.at[core, self.p, self.q_at, (z + o) % 8], dst_ref=self.third_in.at[o - 1],
+                send_sem=self.z_send.at[o - 1], recv_sem=self.z_recv.at[o - 1],
+                device_id=at_z(o), device_id_type=MESH,
+            )
+
+        def along_z(self, i):
+            for j in range(4):
+                o = (4 * i + j + 8 - z) % 8
+
+                @pl.when(o != 0)
+                def start():
+                    self.to_z(o).start()
+
+        def z_copies(self):
+            return [self.to_z(o) for o in range(1, 8)]
 
         def result(self):
-            return last(self.q[core, self.p, self.q_at, z], self.third_in, self.third)
+            return last(self.q[core, self.p, self.q_at, z], self.third_in, self.z_copies())
 
     def last(value, landed, copies):
         for copy in copies:
@@ -365,8 +377,8 @@
             value = value + landed[j]
         return value
 
-    ga = Group(qa, a0, ah, an, af, a2, a3, at_x, at_y, xx, y)
-    gb = Group(qb, b0, bh, bn, bf, b2, b3, at_y, at_x, y, xx)
+    ga = Group(qa, a0, ah, an, af, a2, a3, at_x, at_y, xx, y, za_send, za_recv)
+    gb = Group(qb, b0, bh, bn, bf, b2, b3, at_y, at_x, y, xx, zb_send, zb_recv)
     both = (ga, gb)
 
     def product(k):
@@ -422,15 +434,15 @@
     added(qc.at[core, z, xx], [c2.at[j] for j in range(3)], c_two)
     c_three = [send(qc.at[core, z, xx, (y + o) % 4 // 2], c3.at[o - 1], at_y(o)) for o in (2, 1, 3)]
     each("collect", 0)
+    each("along_z", 0)
     each("collect", 1)
-    for group in both:
-        group.along_z()
+    each("along_z", 1)
     total = last(qc[core, z, xx, b], c3, c_three)
     out[:, 512:] = jnp.where(y_lo == 0, total, pltpu.roll(total, 4, 0))
     out[:, :256] = ga.result()
     out[:, 256:512] = gb.result()
 
-    for copy in sent:
+    for copy in sent + ga.z_copies() + gb.z_copies():
         copy.wait_send()
 
     def drained(c, carry):
@@ -464,6 +476,8 @@
         pltpu.SemaphoreType.DMA((NCHUNK, MEMBERS)), pltpu.SemaphoreType.DMA((NCHUNK, MEMBERS)),
         pltpu.SemaphoreType.DMA((NCHUNK, MEMBERS)), pltpu.SemaphoreType.DMA((NCHUNK, MEMBERS)),
         pltpu.SemaphoreType.DMA((SLOTS,)), pltpu.SemaphoreType.DMA((SLOTS,)),
+        pltpu.SemaphoreType.DMA((7,)), pltpu.SemaphoreType.DMA((7,)),
+        pltpu.SemaphoreType.DMA((7,)), pltpu.SemaphoreType.DMA((7,)),
     ]
 
 

time: 66.3 us -> 62.6 us (0.944)
  Pallas kernels: 64.2 us -> 60.6 us
    pallas_call x1, Pallas kernels: 63.6 us -> 60 us  [shards(): pl.pallas_call(kernel, out_shape=jax.ShapeDtypeStruct((8, 640), F32), in_...]
where the time goes in v5:
time: 62.6 us; the launch traced here: 62.5 us
  Pallas kernels  60.6 us (97%)
  local copies, waits for them, and re-layouts  1.3 us (2%)
  between operations  0.65 us (1%)
    pallas_call x1, Pallas kernels, shards(): pl.pallas_call(kernel, out_shape=jax.ShapeDtypeStruct((8, 640), F32), in_...  60 us
    unnamed x4, local copies, waits for them, and re-layouts  1.3 us

profile of v5, /device:TPU:1, one launch (start us, length us, event | category | flops | bytes accessed | tf_op | source)
XLA Modules:
  0.0 62.5 jit_solution(17925865815813579962)
XLA Ops:
  0.6 0.0 copy-start
  0.6 0.6 %copy-done = s32[1,64]{1,0:T(1,128)S(1)} copy-done((s32[1,64]{1,0:T(1,128)S(1)}, s32[1,64]{1,0:T(1,128)}, u32[]{:S(2)}) %copy-start) | copy-done | bytes 280
  1.3 0.0 copy-start.1
  1.3 0.7 %copy-done.1 = s32[1,64]{1,0:T(1,128)S(1)} copy-done((s32[1,64]{1,0:T(1,128)S(1)}, s32[1,64]{1,0:T(1,128)}, u32[]{:S(2)}) %copy-start.1) | copy-done | bytes 280
  1.9 60.0 %shard_map.77.packed = f32[8,640]{1,0:T(8,128)S(1)} custom-call(bf16[1,1,1024,1024]{3,2,1,0:T(8,128)(2,1)} %lat_hbm.1, bf16[1024,1024]{1,0:T(8,128)(2,1)} %w_in_hbm.1, bf16[112,1024]{1,0:T(8,128)(2,1)} %bitcast.1, bf16[1,128,1792]{2,1,0:T(8,128)(2,1)} %obs_hbm.1, s32[1,64]{1,0:T(1,128)S(1)} %copy-done, s32[1,64]{1,0:T(1,128)S(1)} %copy-done.1), custom_call_target="tpu_custom_call" | custom-call | tf_op jit(solution)/shard_map/pallas_call | solution.py:493
  61.9 0.6 shard_map.78
Async XLA Ops:
  0.6 0.7 %copy-start = (s32[1,64]{1,0:T(1,128)S(1)}, s32[1,64]{1,0:T(1,128)}, u32[]{:S(2)}) copy-start(s32[1,64]{1,0:T(1,128)} %idx_hbm.1) | copy-start | bytes 772
  1.3 0.7 %copy-start.1 = (s32[1,64]{1,0:T(1,128)S(1)}, s32[1,64]{1,0:T(1,128)}, u32[]{:S(2)}) copy-start(s32[1,64]{1,0:T(1,128)} %cnt_hbm.1) | copy-start | bytes 772

commit v6 on v5

--- a/solution.py
+++ b/solution.py
@@ -121,12 +121,16 @@
         out[c, i] = acc
 
 
-def backward_chunk(c, back, own, weight, wo_t, slope, go, gp):
+def grad_chunk(c, back, own, weight, go):
     rows = pl.ds(pl.multiple_of(c * CROWS, CROWS), CROWS)
     pair = jnp.concatenate([unpack_patch(back[c, j]) for j in range(MEMBERS)], axis=0)
     grad = (own[rows, :] - weight[rows, :] * pair).astype(BF16)
     go[rows, :] = grad
-    gh = jnp.dot(grad, wo_t[...], preferred_element_type=F32)
+
+
+def slope_chunk(c, wo_t, slope, go, gp):
+    rows = pl.ds(pl.multiple_of(c * CROWS, CROWS), CROWS)
+    gh = jnp.dot(go[rows, :], wo_t[...], preferred_element_type=F32)
     gp[rows, :] = (gh * slope[rows, :]).astype(BF16)
 
 
@@ -181,13 +185,7 @@
     def at_core():
         return {"tile": xx * 2 + (1 - core)}
 
-    x[...] = jnp.zeros(x.shape, F32)
-    barrier = pltpu.get_barrier_semaphore()
-    peers = [at_member(o) for o in range(1, 16)] + [at_core()] + [at_x(o) for o in range(1, 4)]
-    for peer in peers:
-        pl.semaphore_signal(barrier, inc=1, device_id=peer, device_id_type=MESH)
-    for o in (1, 2, 3):
-        pl.semaphore_signal(barrier, inc=1, device_id=at_y(o), device_id_type=MESH)
+    peers = [at_member(o) for o in ORDER] + [at_core()] + [at_x(o) for o in range(1, 4)]
 
     def load_lat(c):
         rows = pl.ds(pl.multiple_of(c * CROWS, CROWS), CROWS)
@@ -202,15 +200,23 @@
     ]
     load_wo.start()
     load_w.start()
-    for c in range(NCHUNK):
-        load_lat(c).start()
-    for load in later:
-        load.start()
+    load_lat(0).start()
+    x[...] = jnp.zeros(x.shape, F32)
+    barrier = pltpu.get_barrier_semaphore()
+    for peer in peers:
+        pl.semaphore_signal(barrier, inc=1, device_id=peer, device_id_type=MESH)
+    for o in (1, 2, 3):
+        pl.semaphore_signal(barrier, inc=1, device_id=at_y(o), device_id_type=MESH)
     wo_t[CH:, :] = jnp.zeros((LANE - CH, HID), BF16)
     load_wo.wait()
     wo_t[:CH, :] = w_raw[...]
     wo[...] = wo_t[...].T
     load_w.wait()
+    load_lat(0).wait()
+    for c in range(1, NCHUNK):
+        load_lat(c).start()
+    for load in later:
+        load.start()
 
     def there(c, o):
         return pltpu.make_async_remote_copy(
@@ -231,7 +237,6 @@
             make(c, o).wait_recv()
 
     def forward(c, carry):
-        load_lat(c).wait()
         forward_chunk(c, lat, w_in, wo, pre, hid, dec, packed)
         return carry
 
@@ -241,6 +246,7 @@
             there(c, o).start()
 
     def forward_and_depart(c, carry):
+        load_lat(c).wait()
         forward(c, carry)
         depart(c)
         return carry
@@ -271,14 +277,15 @@
 
     def backward(c, carry):
         arrived(returned, c)
-        backward_chunk(c, back, own, weight, wo_t, pre, go, gp)
+        grad_chunk(c, back, own, weight, go)
+        slope_chunk(c, wo_t, pre, go, gp)
         accumulate(c, hid_t, go, sum2)
         accumulate(c, lat_t, gp, sum1)
         return carry
 
     lax.fori_loop(0, NCHUNK - 1, backward, 0)
     arrived(returned, NCHUNK - 1)
-    backward_chunk(NCHUNK - 1, back, own, weight, wo_t, pre, go, gp)
+    grad_chunk(NCHUNK - 1, back, own, weight, go)
 
     slots = iter(range(SLOTS))
     sent = []
@@ -409,6 +416,7 @@
                     qc[core_, 2 * k + j, x_, 0] = c_lo[x_, core_]
                     qc[core_, 2 * k + j, x_, 1] = c_hi[x_, core_]
     c_core = send(qc.at[1 - core], c0, at_core())
+    slope_chunk(NCHUNK - 1, wo_t, pre, go, gp)
     product(0)
     product(1)
     added(qc.at[core], [c0], [c_core])

time: 62.6 us -> 61.3 us (0.979)
  Pallas kernels: 60.6 us -> 58.9 us
    pallas_call x1, Pallas kernels: 60 us -> 58.3 us  [shards(): pl.pallas_call(kernel, out_shape=jax.ShapeDtypeStruct((8, 640), F32), in_...]
where the time goes in v6:
time: 61.3 us; the launch traced here: 60.9 us
  Pallas kernels  58.9 us (96%)
  local copies, waits for them, and re-layouts  1.3 us (2%)
  between operations  0.65 us (1%)
    pallas_call x1, Pallas kernels, shards(): pl.pallas_call(kernel, out_shape=jax.ShapeDtypeStruct((8, 640), F32), in_...  58.3 us
    unnamed x4, local copies, waits for them, and re-layouts  1.3 us

profile of v6, /device:TPU:1, one launch (start us, length us, event | category | flops | bytes accessed | tf_op | source)
XLA Modules:
  0.0 60.9 jit_solution(463181960530933229)
XLA Ops:
  0.6 0.0 copy-start
  0.6 0.6 %copy-done = s32[1,64]{1,0:T(1,128)S(1)} copy-done((s32[1,64]{1,0:T(1,128)S(1)}, s32[1,64]{1,0:T(1,128)}, u32[]{:S(2)}) %copy-start) | copy-done | bytes 280
  1.3 0.0 copy-start.1
  1.3 0.7 %copy-done.1 = s32[1,64]{1,0:T(1,128)S(1)} copy-done((s32[1,64]{1,0:T(1,128)S(1)}, s32[1,64]{1,0:T(1,128)}, u32[]{:S(2)}) %copy-start.1) | copy-done | bytes 280
  1.9 58.3 %shard_map.77.packed = f32[8,640]{1,0:T(8,128)S(1)} custom-call(bf16[1,1,1024,1024]{3,2,1,0:T(8,128)(2,1)} %lat_hbm.1, bf16[1024,1024]{1,0:T(8,128)(2,1)} %w_in_hbm.1, bf16[112,1024]{1,0:T(8,128)(2,1)} %bitcast.1, bf16[1,128,1792]{2,1,0:T(8,128)(2,1)} %obs_hbm.1, s32[1,64]{1,0:T(1,128)S(1)} %copy-done, s32[1,64]{1,0:T(1,128)S(1)} %copy-done.1), custom_call_target="tpu_custom_call" | custom-call | tf_op jit(solution)/shard_map/pallas_call | solution.py:501
  60.3 0.6 %shard_map.78 = (f32[4,1024]{1,0:T(4,128)}, f32[4,112]{1,0:T(4,128)}) custom-call(f32[8,640]{1,0:T(8,128)S(1)} %shard_map.77.packed), custom_call_target="tpu_custom_call" | custom-call | tf_op jit(solution)/shard_map/pallas_call | solution.py:511
Async XLA Ops:
  0.6 0.7 %copy-start = (s32[1,64]{1,0:T(1,128)S(1)}, s32[1,64]{1,0:T(1,128)}, u32[]{:S(2)}) copy-start(s32[1,64]{1,0:T(1,128)} %idx_hbm.1) | copy-start | bytes 772
  1.3 0.7 %copy-start.1 = (s32[1,64]{1,0:T(1,128)S(1)}, s32[1,64]{1,0:T(1,128)}, u32[]{:S(2)}) copy-start(s32[1,64]{1,0:T(1,128)} %cnt_hbm.1) | copy-start | bytes 772

commit v7 on v6

--- a/solution.py
+++ b/solution.py
@@ -431,11 +431,11 @@
     each("first", 3)
     each("relay", 2)
     each("relay", 3)
+    added(qc.at[core, z], [c1.at[j] for j in range(7)], c_one)
+    c_two = [send(qc.at[core, z, (xx + o) % 4], c2.at[o - 1], at_x(o)) for o in (2, 1, 3)]
     each("finish", 0)
     each("finish", 1)
     each("other_ring", 0)
-    added(qc.at[core, z], [c1.at[j] for j in range(7)], c_one)
-    c_two = [send(qc.at[core, z, (xx + o) % 4], c2.at[o - 1], at_x(o)) for o in (2, 1, 3)]
     each("finish", 2)
     each("finish", 3)
     each("other_ring", 1)

time: 61.3 us -> 61.6 us (level)
  no operation moved by 1% of the time
where the time goes in v7:
time: 61.6 us; the launch traced here: 61.5 us
  Pallas kernels  59.5 us (97%)
  local copies, waits for them, and re-layouts  1.3 us (2%)
  between operations  0.65 us (1%)
    pallas_call x1, Pallas kernels, shards(): pl.pallas_call(kernel, out_shape=jax.ShapeDtypeStruct((8, 640), F32), in_...  58.9 us
    unnamed x4, local copies, waits for them, and re-layouts  1.3 us

profile of v7, /device:TPU:1, one launch (start us, length us, event | category | flops | bytes accessed | tf_op | source)
XLA Modules:
  0.0 61.5 jit_solution(7061913791720159711)
XLA Ops:
  0.6 0.0 copy-start
  0.6 0.6 %copy-done = s32[1,64]{1,0:T(1,128)S(1)} copy-done((s32[1,64]{1,0:T(1,128)S(1)}, s32[1,64]{1,0:T(1,128)}, u32[]{:S(2)}) %copy-start) | copy-done | bytes 280
  1.3 0.0 copy-start.1
  1.3 0.7 %copy-done.1 = s32[1,64]{1,0:T(1,128)S(1)} copy-done((s32[1,64]{1,0:T(1,128)S(1)}, s32[1,64]{1,0:T(1,128)}, u32[]{:S(2)}) %copy-start.1) | copy-done | bytes 280
  1.9 58.9 %shard_map.77.packed = f32[8,640]{1,0:T(8,128)S(1)} custom-call(bf16[1,1,1024,1024]{3,2,1,0:T(8,128)(2,1)} %lat_hbm.1, bf16[1024,1024]{1,0:T(8,128)(2,1)} %w_in_hbm.1, bf16[112,1024]{1,0:T(8,128)(2,1)} %bitcast.1, bf16[1,128,1792]{2,1,0:T(8,128)(2,1)} %obs_hbm.1, s32[1,64]{1,0:T(1,128)S(1)} %copy-done, s32[1,64]{1,0:T(1,128)S(1)} %copy-done.1), custom_call_target="tpu_custom_call" | custom-call | tf_op jit(solution)/shard_map/pallas_call | solution.py:501
  60.9 0.6 shard_map.78
Async XLA Ops:
  0.6 0.7 %copy-start = (s32[1,64]{1,0:T(1,128)S(1)}, s32[1,64]{1,0:T(1,128)}, u32[]{:S(2)}) copy-start(s32[1,64]{1,0:T(1,128)} %idx_hbm.1) | copy-start | bytes 772
  1.3 0.7 %copy-start.1 = (s32[1,64]{1,0:T(1,128)S(1)}, s32[1,64]{1,0:T(1,128)}, u32[]{:S(2)}) copy-start(s32[1,64]{1,0:T(1,128)} %cnt_hbm.1) | copy-start | bytes 772
